TPU v7x, 128 devices: a whole 4x4x4 slice. The times are simulated.
128 devices in a mesh: gx: 32 (over x, y, core), gy: 4 (over z).
Axes of the slice: x: 4, y: 4, z: 4, core: 2. Of those that a mesh axis runs over, the one named last changes fastest.
Arguments:
- populations: float32 [19, 128, 128, 256], P(None, 'gx', 'gy'), may hold values from 0.6 to 1.4
- relax_rates: float32 [19], replicated, may hold values from 0.8 to 1.9
- velocity: float32 [3, 65536], P(None, ('gx', 'gy')), may hold values from -0.2 to 0.2
- velocity_change: float32 [3, 65536], P(None, ('gx', 'gy')), may hold values from -0.16 to 0.16
- fractions: float32 [27, 65536], P(None, ('gx', 'gy')), may hold values from 0.05 to 0.5
- anchor: int32 [65536], P(('gx', 'gy')), may hold values from 8449 to 24318, as said below
- destination: int32 [65536], P(('gx', 'gy')), may hold values from 0 to 9, as said below
Outputs:
- advanced: float32 [19, 128, 128, 256], P(None, 'gx', 'gy')
Inputs may be any that keep to these rules, and one draw needn't show every extreme that they name: `destination`: empty rows (9) carry no particle. Every brick sends exactly 4 particles to each of its 8 neighbouring bricks that lie inside the grid across the bed (gy index within 0 to 3; along gx the neighbours wrap around); the rest of the occupied rows stay (4); brick rows at gy index q hold 512 // 2^q occupied rows. Each anchor lies at least one cell inside its destination brick along x, y and z, so that the whole correlation cube lies in that brick.
All inputs are finite; a program needn't handle non-finite values.
Results may differ from a plain program's by a relative error of at most 0.0001.
Values sent between devices are 32-bit elements; how exact they have to be, the bound alone decides.
A program may use at most 128 MiB of HBM per device.

v0:
```python
import jax
import jax.numpy as jnp
import numpy as np
from jax import lax
from jax.sharding import PartitionSpec as P

CAP = 4
STEPS = 2


def padded_2(cells, sides, width):
    for axis, dim in sides:
        count = lax.axis_size(axis)
        head = lax.slice_in_dim(cells, 0, width, axis=dim)
        tail = lax.slice_in_dim(cells, cells.shape[dim] - width, cells.shape[dim], axis=dim)
        cells = jnp.concatenate(
            [
                lax.ppermute(tail, axis, [(i, (i + 1) % count) for i in range(count)]),
                cells,
                lax.ppermute(head, axis, [((i + 1) % count, i) for i in range(count)]),
            ],
            axis=dim,
        )
    return cells


def from_behind(value, axis, steps):
    count = lax.axis_size(axis)
    pairs = [(source, (source + steps) % count) for source in range(count)]
    return lax.ppermute(value, axis, pairs)


def passed_along(value, axis, steps):
    count = lax.axis_size(axis)
    first, last = (max(0, -steps), min(count, count - steps))
    return lax.ppermute(value, axis, [(source, source + steps) for source in range(first, last)])


def lattice():
    vectors = [[0, 0, 0]]
    for axis_one in range(3):
        for orient in (1, -1):
            vector_one = [0, 0, 0]
            vector_one[axis_one] = orient
            vectors.append(vector_one)
    for axis_one, axis_two in ((0, 1), (0, 2), (1, 2)):
        for orient in (1, -1):
            for second in (1, -1):
                vector_one = [0, 0, 0]
                vector_one[axis_one] = orient
                vector_one[axis_two] = second
                vectors.append(vector_one)
    integral = np.array(vectors)
    speeds = integral * 1.0
    length = (speeds**2).sum(axis=1)
    weights = np.where(length == 0, 1.0 / 3.0, np.where(length == 1, 1.0 / 18.0, 1.0 / 36.0))
    opposite = np.array(
        [vectors.index([0 - component for component in vector_one]) for vector_one in vectors]
    )
    along_x, along_y, along_z = (speeds[:, 0], speeds[:, 1], speeds[:, 2])
    rows_list = [
        np.ones(19),
        along_x,
        along_y,
        along_z,
        length,
        3 * along_x**2 - length,
        along_y**2 - along_z**2,
        along_x * along_y,
        along_y * along_z,
        along_x * along_z,
        along_x * length,
        along_y * length,
        along_z * length,
        along_x * (along_y**2 - along_z**2),
        along_y * (along_z**2 - along_x**2),
        along_z * (along_x**2 - along_y**2),
        length**2,
        (3 * along_x**2 - length) * length,
        (along_y**2 - along_z**2) * length,
    ]
    basis_rows = []
    for candidate in rows_list:
        for earlier in basis_rows:
            candidate = candidate - np.dot(candidate, earlier) * earlier
        basis_rows.append(candidate / np.sqrt(np.dot(candidate, candidate)))
    basis = np.array(basis_rows)
    return (speeds, weights, opposite, basis, integral)


def tables():
    speeds, weights, opposite, basis, integral = lattice()
    lattice_vel = jnp.asarray(speeds, jnp.float32)
    moment_rows = jnp.asarray(
        np.concatenate([weights[None, :], (weights[:, None] * speeds).T], axis=0), jnp.float32
    )
    to_moments = jnp.asarray(basis * weights[None, :], jnp.float32)
    from_moments = jnp.asarray(basis.T / weights[:, None], jnp.float32)
    return (lattice_vel, moment_rows, to_moments, from_moments, opposite, integral)


def equilibrium(density, flow, lattice_vel):
    projected = jnp.dot(lattice_vel, flow, precision=lax.Precision.HIGHEST)
    speed_sq = jnp.sum(flow * flow, axis=0)
    return density[None, :] * (
        1.0 + 3.0 * projected + 4.5 * projected * projected - 1.5 * speed_sq[None, :]
    )


def collide(states, solid_part, solid_flow, relax_rates, packed):
    lattice_vel, moment_rows, to_moments, from_moments, opposite = packed
    moments = jnp.dot(moment_rows, states, precision=lax.Precision.HIGHEST)
    density = moments[0]
    flow = moments[1:] / density[None, :]
    fluid_eq = equilibrium(density, flow, lattice_vel)
    solid_eq = equilibrium(density, solid_flow, lattice_vel)
    off_eq = states - fluid_eq
    projected = jnp.dot(to_moments, off_eq, precision=lax.Precision.HIGHEST)
    relaxed = jnp.dot(
        from_moments, relax_rates[:, None] * projected, precision=lax.Precision.HIGHEST
    )
    bounce = states[opposite] - fluid_eq[opposite] - (states - solid_eq)
    return states - (1.0 - solid_part)[None, :] * relaxed + solid_part[None, :] * bounce


def stream(post, speeds, opposite):
    size_x, size_y = (post.shape[1], post.shape[2])
    padded = padded_2(post, (("gx", 1), ("gy", 2)), 1)
    coord_y = (lax.axis_index("gy") * size_y + jnp.arange(size_y, dtype=jnp.int32))[None, :, None]
    last_row = size_y * lax.axis_size("gy") - 1
    read = []
    for number in range(19):
        shift_x, shift_y, shift_z = (
            int(speeds[number, 0]),
            int(speeds[number, 1]),
            int(speeds[number, 2]),
        )
        pulled = padded[
            number, 1 - shift_x : 1 - shift_x + size_x, 1 - shift_y : 1 - shift_y + size_y, :
        ]
        pulled = jnp.roll(pulled, shift_z, axis=2)
        if shift_y == 1:
            pulled = jnp.where(coord_y == 0, post[opposite[number]], pulled)
        elif shift_y == -1:
            pulled = jnp.where(coord_y == last_row, post[opposite[number]], pulled)
        read.append(pulled)
    return jnp.stack(read, axis=0)


def deposit(ids_all, shares, velocities, size_x, size_y, size_z):
    cells = size_x * size_y * size_z
    combined = jnp.concatenate(
        [shares[None, :, :], shares[None, :, :] * velocities[:, None, :]], axis=0
    )
    row_values = jnp.transpose(combined, (2, 1, 0)).reshape(combined.shape[2], 108)
    target = jnp.clip(ids_all, 0, cells - 1)
    centred = jnp.zeros((cells, 108), jnp.float32).at[target].add(row_values)
    field = centred.reshape(size_x, size_y, size_z, 108)
    padded = jnp.pad(field, ((1, 1), (1, 1), (1, 1), (0, 0)))
    total = jnp.zeros((size_x, size_y, size_z, 4), jnp.float32)
    for offset in range(27):
        move_x, move_y, move_z = (offset // 9 - 1, offset // 3 % 3 - 1, offset % 3 - 1)
        total = (
            total
            + padded[
                1 - move_x : 1 - move_x + size_x,
                1 - move_y : 1 - move_y + size_y,
                1 - move_z : 1 - move_z + size_z,
                4 * offset : 4 * offset + 4,
            ]
        )
    gathered = jnp.transpose(total.reshape(cells, 4), (1, 0))
    return (gathered[0], gathered[1:])


def local(populations, relax_rates, velocity, velocity_change, fractions, anchor, destination):
    lattice_vel, moment_rows, to_moments, from_moments, opposite, speeds = tables()
    packed = (lattice_vel, moment_rows, to_moments, from_moments, opposite)
    size_x, size_y, size_z = (populations.shape[1], populations.shape[2], populations.shape[3])
    cells = size_x * size_y * size_z
    new_velocity = velocity + velocity_change
    payload = jnp.concatenate([new_velocity, fractions], axis=0)
    width_rows = payload.shape[0]
    anchors = anchor[None, :]
    labels = jnp.arange(10, dtype=jnp.int32)
    one_hot = (destination[:, None] == labels[None, :]).astype(jnp.int32)
    ranking = jnp.sum(jnp.cumsum(one_hot, axis=0) * one_hot, axis=1) - 1
    leaving = (destination < 9) & (destination != 4)
    staying = destination == 4
    placed = jnp.where(leaving, destination * CAP + ranking, 9 * CAP)
    outgoing = jnp.zeros((width_rows, 9 * CAP), jnp.float32).at[:, placed].set(payload, mode="drop")
    outgoing = outgoing.reshape(width_rows, 3, 3, CAP)
    outgoing_ids = jnp.zeros((1, 9 * CAP), jnp.int32).at[:, placed].set(anchors, mode="drop")
    outgoing_ids = outgoing_ids.reshape(1, 3, 3, CAP)
    column_parts = [outgoing[:, 1]]
    column_idparts = [outgoing_ids[:, 1]]
    for orient in (1, -1):
        moved, moved_ids = from_behind(
            (outgoing[:, 1 + orient], outgoing_ids[:, 1 + orient]), "gx", orient
        )
        column_parts.append(moved)
        column_idparts.append(moved_ids)
    columns = jnp.concatenate(column_parts, axis=2)
    column_ids = jnp.concatenate(column_idparts, axis=2)
    arrived_parts = [columns[:, 1]]
    arrived_idparts = [column_ids[:, 1]]
    for orient in (1, -1):
        moved, moved_ids = passed_along(
            (columns[:, 1 + orient], column_ids[:, 1 + orient]), "gy", orient
        )
        arrived_parts.append(moved)
        arrived_idparts.append(moved_ids)
    arrived = jnp.concatenate(arrived_parts, axis=1)
    arrived_ids = jnp.concatenate(arrived_idparts, axis=1)
    rows_all = jnp.concatenate([payload, arrived], axis=1)
    ids_all = jnp.concatenate([anchor, arrived_ids[0]], axis=0)
    keep = jnp.concatenate([staying, jnp.ones((arrived.shape[1],), jnp.bool_)], axis=0)
    shares = jnp.where(keep[None, :], rows_all[3:], jnp.float32(0.0))
    solid_sum, momentum = deposit(ids_all, shares, rows_all[:3], size_x, size_y, size_z)
    solid = jnp.minimum(solid_sum, 1.0)
    solid_velocity = momentum / (solid_sum + 1e-06)[None, :]
    states = populations.reshape(19, cells)
    for sweep_number in range(STEPS):
        post = collide(states, solid, solid_velocity, relax_rates, packed)
        states = stream(post.reshape(19, size_x, size_y, size_z), speeds, opposite).reshape(
            19, cells
        )
    return states.reshape(19, size_x, size_y, size_z)


def solution(mesh):
    placed = (
        P(None, "gx", "gy", None),
        P(),
        P(None, ("gx", "gy")),
        P(None, ("gx", "gy")),
        P(None, ("gx", "gy")),
        P(("gx", "gy")),
        P(("gx", "gy")),
    )
    return jax.shard_map(
        local, mesh=mesh, in_specs=placed, out_specs=P(None, "gx", "gy", None), check_vma=False
    )
```

profile of v0, /device:TPU:0, one launch (start us, length us, event | category | flops | bytes accessed | tf_op | source)
XLA Modules:
  0.0 381.3 jit_solution(7780644710038189138)
XLA Ops:
  5.3 1.7 scatter_custom_fusion.1
  7.1 5.1 %collective-permute-start.5 = (f32[30,3,4]{0,2,1:T(4,128)S(1)}, f32[30,3,4]{0,2,1:T(4,128)S(1)}, u32[]{:S(2)}, u32[]{:S(2)}) collective-permute-start(f32[30,3,4]{0,2,1:T(4,128)S(1)} %get-tuple-element.96), channel_id=1, source_target_pairs={{0,124},{4,0},{8,4},{12,8},{16,12},{20,16},{24,20},{28,24},{32,28}... | collective-permute-start | bytes 4328 | tf_op jit(solution)/shard_map/ppermute | solution.py:30
  12.2 2.6 scatter_custom_fusion
  15.0 5.2 %collective-permute-start.1 = (s32[1,3,4]{2,0,1:T(1,128)S(1)}, s32[1,3,4]{2,0,1:T(1,128)}, u32[]{:S(2)}, u32[]{:S(2)}) collective-permute-start(s32[1,3,4]{2,0,1:T(1,128)S(1)} %squeeze.170), channel_id=1, source_target_pairs={{0,124},{4,0},{8,4},{12,8},{16,12},{20,16},{24,20},{28,24},{32,28}... | collective-permute-start | bytes 152 | tf_op jit(solution)/shard_map/ppermute | solution.py:30
  20.9 2.0 pad.123
  22.9 1.8 copy.63
  24.8 1.7 fusion.79
  28.5 2.8 gather_fusion
  31.4 5.8 %fusion.36 = f32[19,32768]{1,0:T(8,128)} fusion(f32[19,3]{1,0:T(8,128)S(1)} %copy-done.70, f32[32768]{0:T(1024)S(1)} %copy-done.39, f32[32768]{0:T(1024)S(1)} %bitcast.271, f32[4,32768]{1,0:T(4,128)} %copy-done.8), kind=kOutput, calls=%fused_computation.76 | convolution fusion | flops 26869760 | bytes 3420160 | tf_op jit(solution)/shard_map/dot_general | solution.py:103
  37.2 5.9 %gather_fusion.1 = f32[19,32768]{1,0:T(8,128)} fusion(f32[19,32768]{1,0:T(8,128)} %fusion.36, s32[1024]{0:T(1024)S(1)} %pad_clamp_fusion), kind=kCustom, calls=%fused_computation.1 | custom fusion | bytes 4980812 | tf_op jit(solution)/shard_map/gather | solution.py:122
  44.7 6.8 %convolution_multiply_fusion.3 = f32[32768,19]{0,1:T(8,128)} fusion(f32[19,19]{1,0:T(8,128)S(1)} %copy-done.41, f32[19,32768]{1,0:T(8,128)S(1)} %bitcast.249, f32[19,32768]{1,0:T(8,128)} %fusion.36, f32[19]{0:T(128)S(1)} %copy-done.48), kind=kOutput, calls=%fused_computation.42 | convolution fusion | flops 143196160 | bytes 7472624 | tf_op jit(solution)/shard_map/dot_general | solution.py:118
  52.3 3.9 %collective-permute-start.2 = (s32[1,12]{1,0:T(1,128)S(1)}, s32[1,12]{1,0:T(1,128)S(1)}, u32[]{:S(2)}, u32[]{:S(2)}) collective-permute-start(s32[1,12]{1,0:T(1,128)S(1)} %get-tuple-element.103), channel_id=1, source_target_pairs={{0,1},{1,2},{2,3},{4,5},{5,6},{6,7},{8,9},{9,10},{10,11},{12,13},{... | collective-permute-start | bytes 152 | tf_op jit(solution)/shard_map/ppermute | solution.py:36
  57.5 4.5 %collective-permute-start.6 = (f32[30,12]{0,1:T(8,128)S(1)}, f32[30,12]{0,1:T(8,128)S(1)}, u32[]{:S(2)}, u32[]{:S(2)}) collective-permute-start(f32[30,12]{0,1:T(8,128)S(1)} %get-tuple-element.94), channel_id=1, source_target_pairs={{0,1},{1,2},{2,3},{4,5},{5,6},{6,7},{8,9},{9,10},{10,11},{12,13},{... | collective-permute-start | bytes 4328 | tf_op jit(solution)/shard_map/ppermute | solution.py:36
  63.7 3.9 %collective-permute-done.7 = f32[30,12]{0,1:T(8,128)S(1)} collective-permute-done((f32[30,12]{0,1:T(8,128)S(1)}, f32[30,12]{0,1:T(8,128)S(1)}, u32[]{:S(2)}, u32[]{:S(2)}) %collective-permute-start.7) | collective-permute-done | bytes 1472 | tf_op jit(solution)/shard_map/ppermute | solution.py:36
  68.9 1.8 reshape.481
  70.7 1.8 copy.52
  72.5 13.4 %scatter_custom_fusion.2 = f32[32768,108]{1,0:T(8,128)} fusion(s32[548]{0:T(1024)S(1)} %fusion.69, f32[548,108]{1,0:T(8,128)} %copy.52, f32[]{:T(128)} %constant.25.clone.1), kind=kCustom, calls=%fused_computation.69 | custom fusion | flops 59184 | bytes 14156288 | tf_op jit(solution)/shard_map/scatter-add | solution.py:157
  85.9 139.0 %fusion.31 = f32[4,32,256,4]{3,2,1,0:T(8,128)} fusion(f32[4,32,256,108]{3,2,1,0:T(8,128)} %bitcast.251), kind=kLoop, calls=%fused_computation.68 | loop fusion | flops 3407872 | bytes 34078720 | tf_op jit(solution)/shard_map/add | solution.py:164
  224.9 10.3 %copy.62 = f32[32768,4]{0,1:T(4,128)} copy(f32[32768,4]{1,0:T(8,128)} %bitcast.252) | data formatting | bytes 1048576 | tf_op jit(solution)/shard_map/reshape | solution.py:172
  236.5 1.7 multiply_reduce_fusion.1
  238.3 4.3 %fusion.38 = f32[19,32768]{1,0:T(8,128)S(1)} fusion(f32[19,3]{1,0:T(8,128)} %constant.20.clone, f32[32768]{0:T(1024)S(1)} %broadcast_multiply_fusion.2, f32[4,32768]{1,0:T(4,128)} %bitcast.264, f32[32768]{0:T(1024)S(1)} %bitcast.340), kind=kOutput, calls=%fused_computation.78 | convolution fusion | flops 26247168 | bytes 3277028 | tf_op jit(solution)/shard_map/dot_general | solution.py:103
  242.6 4.1 %fusion.5 = f32[19,32768]{1,0:T(8,128)S(1)} fusion(f32[19,32768]{1,0:T(8,128)S(1)} %bitcast.250, f32[32768,19]{0,1:T(8,128)S(1)} %copy-done.5, f32[19,19]{1,0:T(8,128)S(1)} %copy-done.40, f32[19,32768]{1,0:T(8,128)S(1)} %fusion.38, f32[19,32768]{1,0:T(8,128)S(1)} %copy-done.6, f32[19,32768]{1,0:T(8,128)S(1)} %copy-done.7, f32[32768]{0:T(1024)S(1)} %bitcast.268, ...), kind=kOutput, calls=%fused_computation.41 | convolution fusion | flops 146931712 | bytes 15336868 | tf_op jit(solution)/shard_map/dot_general | solution.py:119
  249.3 3.5 slice_reduce_fusion.13
  253.0 5.1 %collective-permute-start.9 = (f32[19,1,32,256]{3,2,1,0:T(8,128)}, f32[19,1,32,256]{3,2,1,0:T(8,128)}, u32[]{:S(2)}, u32[]{:S(2)}) collective-permute-start(f32[19,1,32,256]{3,2,1,0:T(8,128)} %get-tuple-element.79), channel_id=1, source_target_pairs={{4,0},{8,4},{12,8},{16,12},{20,16},{24,20},{28,24},{32,28},{36,32}... | collective-permute-start | bytes 1867784 | tf_op jit(solution)/shard_map/ppermute | solution.py:20
  261.0 1.6 squeeze.180
  264.2 1.6 squeeze.186
  272.0 2.0 collective-permute-start.10
  277.9 1.6 collective-permute-start.11
  285.1 3.5 slice_select_fusion
  291.0 3.2 fusion.41
  294.1 3.0 gather_fusion.3
  297.1 1.7 copy.72
  298.8 1.7 copy.68
  300.5 1.7 copy.70
  302.2 1.7 copy.71
  303.9 1.7 copy.73
  305.5 1.7 copy.69
  307.2 8.2 %stack.98 = f32[19,32768]{1,0:T(8,128)S(1)} concatenate(f32[1,32768]{1,0:T(1,128)} %copy-done.13, f32[1,32768]{1,0:T(1,128)} %bitcast.312, f32[1,32768]{1,0:T(1,128)} %bitcast.311, f32[1,32768]{1,0:T(1,128)} %bitcast.329, f32[1,32768]{1,0:T(1,128)} %bitcast.334, f32[1,32768]{1,0:T(1,128)} %stack.88, f32[1,32768]{1,0:T(1,128)} %stack.89, f32[1,32768]{1,0:T(1,128)} %bitcast.330, ...), dimensions={0} | concatenate | bytes 4980736 | tf_op jit(solution)/shard_map/stack | solution.py:147
  315.4 6.7 %convolution_multiply_fusion.1 = f32[32768,19]{0,1:T(8,128)} fusion(f32[19,19]{1,0:T(8,128)} %constant.22.clone, f32[19,32768]{1,0:T(8,128)S(1)} %stack.98, f32[19,32768]{1,0:T(8,128)} %copy-done, f32[19]{0:T(128)} %param.17), kind=kOutput, calls=%fused_computation.37 | convolution fusion | flops 143196160 | bytes 7472624 | tf_op jit(solution)/shard_map/dot_general | solution.py:118
  322.1 3.1 gather_fusion.2
  325.1 8.2 %fusion.2 = f32[19,32768]{1,0:T(8,128)S(1)} fusion(f32[19,32768]{1,0:T(8,128)S(1)} %stack.98, f32[32768,19]{0,1:T(8,128)} %convolution_multiply_fusion.1, f32[19,19]{1,0:T(8,128)S(1)} %copy-done.40, f32[19,32768]{1,0:T(8,128)} %copy-done.4, f32[19,32768]{1,0:T(8,128)} %gather_fusion.2, f32[19,32768]{1,0:T(8,128)} %gather_fusion.3, f32[32768]{0:T(1024)S(1)} %bitcast.275, ...), kind=kOutput, calls=%fused_computation.36 | convolution fusion | flops 146931712 | bytes 15336868 | tf_op jit(solution)/shard_map/dot_general | solution.py:119
  335.6 5.3 %collective-permute-start.13 = (f32[19,1,32,256]{3,2,1,0:T(8,128)S(1)}, f32[19,1,32,256]{3,2,1,0:T(8,128)}, u32[]{:S(2)}, u32[]{:S(2)}) collective-permute-start(f32[19,1,32,256]{3,2,1,0:T(8,128)S(1)} %get-tuple-element.74), channel_id=1, source_target_pairs={{4,0},{8,4},{12,8},{16,12},{20,16},{24,20},{28,24},{32,28},{36,32}... | collective-permute-start | bytes 1867784 | tf_op jit(solution)/shard_map/ppermute | solution.py:20
  340.9 5.0 %slice_reduce_fusion = (f32[32768]{0:T(1024)}, f32[32768]{0:T(1024)}, f32[32768]{0:T(1024)}, f32[32768]{0:T(1024)}, f32[32768]{0:T(1024)}, /*index=5*/f32[32768]...) fusion(f32[19,32768]{1,0:T(8,128)S(1)} %fusion.2), kind=kLoop, calls=%fused_computation.114 | loop fusion | bytes 3407872 | tf_op jit(solution)/shard_map/slice | solution.py:145
  354.7 1.6 squeeze.201
  362.7 1.6 squeeze.214
  368.9 1.7 collective-permute-start.14
  370.9 1.7 collective-permute-start.15
  372.7 2.3 collective-permute-done.14
  (340 shorter events, 68.3 us)
Async XLA Ops:
  7.1 50.4 %collective-permute-start.4 = (f32[30,3,4]{0,2,1:T(4,128)S(1)}, f32[30,3,4]{0,2,1:T(4,128)S(1)}, u32[]{:S(2)}, u32[]{:S(2)}) collective-permute-start(f32[30,3,4]{0,2,1:T(4,128)S(1)} %get-tuple-element.97), channel_id=1, source_target_pairs={{0,4},{4,8},{8,12},{12,16},{16,20},{20,24},{24,28},{28,32},{32,36}... | collective-permute-start | bytes 4328 | tf_op jit(solution)/shard_map/ppermute | solution.py:30
  7.1 50.4 %collective-permute-start.5 = (f32[30,3,4]{0,2,1:T(4,128)S(1)}, f32[30,3,4]{0,2,1:T(4,128)S(1)}, u32[]{:S(2)}, u32[]{:S(2)}) collective-permute-start(f32[30,3,4]{0,2,1:T(4,128)S(1)} %get-tuple-element.96), channel_id=1, source_target_pairs={{0,124},{4,0},{8,4},{12,8},{16,12},{20,16},{24,20},{28,24},{32,28}... | collective-permute-start | bytes 4328 | tf_op jit(solution)/shard_map/ppermute | solution.py:30
  14.9 36.6 %collective-permute-start = (s32[1,3,4]{2,0,1:T(1,128)S(1)}, s32[1,3,4]{2,0,1:T(1,128)S(1)}, u32[]{:S(2)}, u32[]{:S(2)}) collective-permute-start(s32[1,3,4]{2,0,1:T(1,128)S(1)} %squeeze.169), channel_id=1, source_target_pairs={{0,4},{4,8},{8,12},{12,16},{16,20},{20,24},{24,28},{28,32},{32,36}... | collective-permute-start | bytes 152 | tf_op jit(solution)/shard_map/ppermute | solution.py:30
  15.0 36.5 %collective-permute-start.1 = (s32[1,3,4]{2,0,1:T(1,128)S(1)}, s32[1,3,4]{2,0,1:T(1,128)}, u32[]{:S(2)}, u32[]{:S(2)}) collective-permute-start(s32[1,3,4]{2,0,1:T(1,128)S(1)} %squeeze.170), channel_id=1, source_target_pairs={{0,124},{4,0},{8,4},{12,8},{16,12},{20,16},{24,20},{28,24},{32,28}... | collective-permute-start | bytes 152 | tf_op jit(solution)/shard_map/ppermute | solution.py:30
  20.9 22.2 %copy-start.42 = (pred[32]{0:T(512)(128)(4,1)}, pred[32]{0:T(512)(128)(4,1)S(1)}, u32[]{:S(2)}) copy-start(pred[32]{0:T(512)(128)(4,1)S(1)} %fusion.71) | copy-start | bytes 100
  28.5 8.7 %copy-start.45 = (s32[1024]{0:T(1024)}, s32[1024]{0:T(1024)S(1)}, u32[]{:S(2)}) copy-start(s32[1024]{0:T(1024)S(1)} %pad_clamp_fusion) | copy-start | bytes 12292
  37.2 7.5 %copy-start.41 = (f32[19,19]{1,0:T(8,128)S(1)}, f32[19,19]{1,0:T(8,128)}, u32[]{:S(2)}) copy-start(f32[19,19]{1,0:T(8,128)} %constant.22.clone) | copy-start | bytes 4336
  37.2 7.5 %copy-start.48 = (f32[19]{0:T(128)S(1)}, f32[19]{0:T(128)}, u32[]{:S(2)}) copy-start(f32[19]{0:T(128)} %param.17) | copy-start | bytes 232
  44.6 18.9 %copy-start.49 = (s32[512]{0:T(512)S(1)}, s32[512]{0:T(512)}, u32[]{:S(2)}) copy-start(s32[512]{0:T(512)} %param.21) | copy-start | bytes 6148
  44.7 23.1 %copy-start.21 = (f32[27,512]{1,0:T(8,128)S(1)}, f32[27,512]{1,0:T(8,128)}, u32[]{:S(2)}) copy-start(f32[27,512]{1,0:T(8,128)} %param.20) | copy-start | bytes 165892
  52.3 11.1 %collective-permute-start.2 = (s32[1,12]{1,0:T(1,128)S(1)}, s32[1,12]{1,0:T(1,128)S(1)}, u32[]{:S(2)}, u32[]{:S(2)}) collective-permute-start(s32[1,12]{1,0:T(1,128)S(1)} %get-tuple-element.103), channel_id=1, source_target_pairs={{0,1},{1,2},{2,3},{4,5},{5,6},{6,7},{8,9},{9,10},{10,11},{12,13},{... | collective-permute-start | bytes 152 | tf_op jit(solution)/shard_map/ppermute | solution.py:36
  56.2 7.2 %collective-permute-start.3 = (s32[1,12]{1,0:T(1,128)S(1)}, s32[1,12]{1,0:T(1,128)S(1)}, u32[]{:S(2)}, u32[]{:S(2)}) collective-permute-start(s32[1,12]{1,0:T(1,128)S(1)} %get-tuple-element.102), channel_id=1, source_target_pairs={{1,0},{2,1},{3,2},{5,4},{6,5},{7,6},{9,8},{10,9},{11,10},{13,12},{... | collective-permute-start | bytes 152 | tf_op jit(solution)/shard_map/ppermute | solution.py:36
  57.5 6.1 %collective-permute-start.6 = (f32[30,12]{0,1:T(8,128)S(1)}, f32[30,12]{0,1:T(8,128)S(1)}, u32[]{:S(2)}, u32[]{:S(2)}) collective-permute-start(f32[30,12]{0,1:T(8,128)S(1)} %get-tuple-element.94), channel_id=1, source_target_pairs={{0,1},{1,2},{2,3},{4,5},{5,6},{6,7},{8,9},{9,10},{10,11},{12,13},{... | collective-permute-start | bytes 4328 | tf_op jit(solution)/shard_map/ppermute | solution.py:36
  62.1 5.5 %collective-permute-start.7 = (f32[30,12]{0,1:T(8,128)S(1)}, f32[30,12]{0,1:T(8,128)S(1)}, u32[]{:S(2)}, u32[]{:S(2)}) collective-permute-start(f32[30,12]{0,1:T(8,128)S(1)} %get-tuple-element.93), channel_id=1, source_target_pairs={{1,0},{2,1},{3,2},{5,4},{6,5},{7,6},{9,8},{10,9},{11,10},{13,12},{... | collective-permute-start | bytes 4328 | tf_op jit(solution)/shard_map/ppermute | solution.py:36
  236.5 6.1 %copy-start.7 = (f32[19,32768]{1,0:T(8,128)S(1)}, f32[19,32768]{1,0:T(8,128)}, u32[]{:S(2)}) copy-start(f32[19,32768]{1,0:T(8,128)} %gather_fusion.1) | copy-start | bytes 7471108
  249.2 17.4 %collective-permute-start.8 = (f32[19,1,32,256]{3,2,1,0:T(8,128)}, f32[19,1,32,256]{3,2,1,0:T(8,128)}, u32[]{:S(2)}, u32[]{:S(2)}) collective-permute-start(f32[19,1,32,256]{3,2,1,0:T(8,128)} %get-tuple-element.80), channel_id=1, source_target_pairs={{0,4},{4,8},{8,12},{12,16},{16,20},{20,24},{24,28},{28,32},{32,36}... | collective-permute-start | bytes 1867784 | tf_op jit(solution)/shard_map/ppermute | solution.py:18
  253.0 15.8 %collective-permute-start.9 = (f32[19,1,32,256]{3,2,1,0:T(8,128)}, f32[19,1,32,256]{3,2,1,0:T(8,128)}, u32[]{:S(2)}, u32[]{:S(2)}) collective-permute-start(f32[19,1,32,256]{3,2,1,0:T(8,128)} %get-tuple-element.79), channel_id=1, source_target_pairs={{4,0},{8,4},{12,8},{16,12},{20,16},{24,20},{28,24},{32,28},{36,32}... | collective-permute-start | bytes 1867784 | tf_op jit(solution)/shard_map/ppermute | solution.py:20
  270.1 11.1 %copy-start.25 = (f32[1,4,32,256]{3,2,1,0:T(8,128)S(1)}, f32[1,4,32,256]{3,2,1,0:T(8,128)}, u32[]{:S(2)}) copy-start(f32[1,4,32,256]{3,2,1,0:T(8,128)} %squeeze.180) | copy-start | bytes 393220
  270.2 11.1 %copy-start.26 = (f32[1,4,32,256]{3,2,1,0:T(8,128)S(1)}, f32[1,4,32,256]{3,2,1,0:T(8,128)}, u32[]{:S(2)}) copy-start(f32[1,4,32,256]{3,2,1,0:T(8,128)} %squeeze.184) | copy-start | bytes 393220
  270.2 11.1 %copy-start.27 = (f32[1,4,32,256]{3,2,1,0:T(8,128)S(1)}, f32[1,4,32,256]{3,2,1,0:T(8,128)}, u32[]{:S(2)}) copy-start(f32[1,4,32,256]{3,2,1,0:T(8,128)} %squeeze.186) | copy-start | bytes 393220
  270.2 11.1 %copy-start.43 = (pred[32]{0:T(512)(128)(4,1)S(1)}, pred[32]{0:T(512)(128)(4,1)}, u32[]{:S(2)}) copy-start(pred[32]{0:T(512)(128)(4,1)} %copy-done.42) | copy-start | bytes 100
  272.0 9.3 %collective-permute-start.10 = (f32[19,6,1,256]{3,2,1,0:T(1,128)S(1)}, f32[19,6,1,256]{3,2,1,0:T(1,128)S(1)}, u32[]{:S(2)}, u32[]{:S(2)}) collective-permute-start(f32[19,6,1,256]{3,2,1,0:T(1,128)S(1)} %get-tuple-element.51), channel_id=1, source_target_pairs={{0,1},{1,2},{2,3},{3,0},{4,5},{5,6},{6,7},{7,4},{8,9},{9,10},{10,1... | collective-permute-start | bytes 350216 | tf_op jit(solution)/shard_map/ppermute | solution.py:18
  277.9 5.1 %collective-permute-start.11 = (f32[19,6,1,256]{3,2,1,0:T(1,128)S(1)}, f32[19,6,1,256]{3,2,1,0:T(1,128)S(1)}, u32[]{:S(2)}, u32[]{:S(2)}) collective-permute-start(f32[19,6,1,256]{3,2,1,0:T(1,128)S(1)} %get-tuple-element.50), channel_id=1, source_target_pairs={{1,0},{2,1},{3,2},{0,3},{5,4},{6,5},{7,6},{4,7},{9,8},{10,9},{11,1... | collective-permute-start | bytes 350216 | tf_op jit(solution)/shard_map/ppermute | solution.py:20
  283.2 5.4 %copy-start.50 = (f32[4]{0:T(128)S(1)}, f32[4]{0:T(128)}, u32[]{:S(2)}) copy-start(f32[4]{0:T(128)} %constant.101) | copy-start | bytes 52
  283.2 5.4 %copy-start.51 = (f32[4]{0:T(128)S(1)}, f32[4]{0:T(128)}, u32[]{:S(2)}) copy-start(f32[4]{0:T(128)} %constant.103) | copy-start | bytes 52
  283.3 5.4 %copy-start.52 = (f32[4]{0:T(128)S(1)}, f32[4]{0:T(128)}, u32[]{:S(2)}) copy-start(f32[4]{0:T(128)} %constant.105) | copy-start | bytes 52
  283.3 5.4 %copy-start.53 = (f32[4]{0:T(128)S(1)}, f32[4]{0:T(128)}, u32[]{:S(2)}) copy-start(f32[4]{0:T(128)} %constant.107) | copy-start | bytes 52
  283.3 5.4 %copy-start.54 = (f32[4]{0:T(128)S(1)}, f32[4]{0:T(128)}, u32[]{:S(2)}) copy-start(f32[4]{0:T(128)} %constant.109) | copy-start | bytes 52
  283.3 5.4 %copy-start.55 = (f32[4]{0:T(128)S(1)}, f32[4]{0:T(128)}, u32[]{:S(2)}) copy-start(f32[4]{0:T(128)} %constant.111) | copy-start | bytes 52
  283.3 5.4 %copy-start.56 = (f32[4]{0:T(128)S(1)}, f32[4]{0:T(128)}, u32[]{:S(2)}) copy-start(f32[4]{0:T(128)} %constant.113) | copy-start | bytes 52
  283.3 5.3 %copy-start.57 = (f32[4]{0:T(128)S(1)}, f32[4]{0:T(128)}, u32[]{:S(2)}) copy-start(f32[4]{0:T(128)} %constant.77) | copy-start | bytes 52
  283.3 5.3 %copy-start.58 = (f32[4]{0:T(128)S(1)}, f32[4]{0:T(128)}, u32[]{:S(2)}) copy-start(f32[4]{0:T(128)} %constant.79) | copy-start | bytes 52
  283.3 5.3 %copy-start.59 = (f32[4]{0:T(128)S(1)}, f32[4]{0:T(128)}, u32[]{:S(2)}) copy-start(f32[4]{0:T(128)} %constant.81) | copy-start | bytes 52
  283.4 5.3 %copy-start.60 = (f32[4]{0:T(128)S(1)}, f32[4]{0:T(128)}, u32[]{:S(2)}) copy-start(f32[4]{0:T(128)} %constant.83) | copy-start | bytes 52
  283.4 5.3 %copy-start.61 = (f32[4]{0:T(128)S(1)}, f32[4]{0:T(128)}, u32[]{:S(2)}) copy-start(f32[4]{0:T(128)} %constant.85) | copy-start | bytes 52
  283.4 5.3 %copy-start.62 = (f32[4]{0:T(128)S(1)}, f32[4]{0:T(128)}, u32[]{:S(2)}) copy-start(f32[4]{0:T(128)} %constant.87) | copy-start | bytes 52
  283.4 5.3 %copy-start.63 = (f32[4]{0:T(128)S(1)}, f32[4]{0:T(128)}, u32[]{:S(2)}) copy-start(f32[4]{0:T(128)} %constant.89) | copy-start | bytes 52
  283.4 5.3 %copy-start.64 = (f32[4]{0:T(128)S(1)}, f32[4]{0:T(128)}, u32[]{:S(2)}) copy-start(f32[4]{0:T(128)} %constant.91) | copy-start | bytes 52
  283.4 5.3 %copy-start.65 = (f32[4]{0:T(128)S(1)}, f32[4]{0:T(128)}, u32[]{:S(2)}) copy-start(f32[4]{0:T(128)} %constant.93) | copy-start | bytes 52
  283.4 5.3 %copy-start.66 = (f32[4]{0:T(128)S(1)}, f32[4]{0:T(128)}, u32[]{:S(2)}) copy-start(f32[4]{0:T(128)} %constant.95) | copy-start | bytes 52
  285.1 5.9 %copy-start.71 = (f32[19,3]{1,0:T(8,128)S(1)}, f32[19,3]{1,0:T(8,128)}, u32[]{:S(2)}) copy-start(f32[19,3]{1,0:T(8,128)} %constant.20.clone) | copy-start | bytes 688
  335.5 29.7 %collective-permute-start.12 = (f32[19,1,32,256]{3,2,1,0:T(8,128)}, f32[19,1,32,256]{3,2,1,0:T(8,128)}, u32[]{:S(2)}, u32[]{:S(2)}) collective-permute-start(f32[19,1,32,256]{3,2,1,0:T(8,128)} %get-tuple-element.75), channel_id=1, source_target_pairs={{0,4},{4,8},{8,12},{12,16},{16,20},{20,24},{24,28},{28,32},{32,36}... | collective-permute-start | bytes 1867784 | tf_op jit(solution)/shard_map/ppermute | solution.py:18
  335.6 31.9 %collective-permute-start.13 = (f32[19,1,32,256]{3,2,1,0:T(8,128)S(1)}, f32[19,1,32,256]{3,2,1,0:T(8,128)}, u32[]{:S(2)}, u32[]{:S(2)}) collective-permute-start(f32[19,1,32,256]{3,2,1,0:T(8,128)S(1)} %get-tuple-element.74), channel_id=1, source_target_pairs={{4,0},{8,4},{12,8},{16,12},{20,16},{24,20},{28,24},{32,28},{36,32}... | collective-permute-start | bytes 1867784 | tf_op jit(solution)/shard_map/ppermute | solution.py:20
  346.9 20.6 %copy-start.20 = (f32[4,32,256]{2,1,0:T(8,128)}, f32[4,32,256]{2,1,0:T(8,128)S(1)}, u32[]{:S(2)}) copy-start(f32[4,32,256]{2,1,0:T(8,128)S(1)} %squeeze.199) | copy-start | bytes 393220
  367.5 7.5 %copy-start.32 = (f32[1,4,32,256]{3,2,1,0:T(8,128)S(1)}, f32[1,4,32,256]{3,2,1,0:T(8,128)}, u32[]{:S(2)}) copy-start(f32[1,4,32,256]{3,2,1,0:T(8,128)} %squeeze.196) | copy-start | bytes 393220
  367.5 7.5 %copy-start.44 = (pred[32]{0:T(512)(128)(4,1)S(1)}, pred[32]{0:T(512)(128)(4,1)}, u32[]{:S(2)}) copy-start(pred[32]{0:T(512)(128)(4,1)} %copy-done.42) | copy-start | bytes 100
  368.9 6.1 %collective-permute-start.14 = (f32[19,6,1,256]{3,2,1,0:T(1,128)S(1)}, f32[19,6,1,256]{3,2,1,0:T(1,128)S(1)}, u32[]{:S(2)}, u32[]{:S(2)}) collective-permute-start(f32[19,6,1,256]{3,2,1,0:T(1,128)S(1)} %get-tuple-element.49), channel_id=1, source_target_pairs={{0,1},{1,2},{2,3},{3,0},{4,5},{5,6},{6,7},{7,4},{8,9},{9,10},{10,1... | collective-permute-start | bytes 350216 | tf_op jit(solution)/shard_map/ppermute | solution.py:18
  370.9 4.9 %collective-permute-start.15 = (f32[19,6,1,256]{3,2,1,0:T(1,128)S(1)}, f32[19,6,1,256]{3,2,1,0:T(1,128)S(1)}, u32[]{:S(2)}, u32[]{:S(2)}) collective-permute-start(f32[19,6,1,256]{3,2,1,0:T(1,128)S(1)} %get-tuple-element.48), channel_id=1, source_target_pairs={{1,0},{2,1},{3,2},{0,3},{5,4},{6,5},{7,6},{4,7},{9,8},{10,9},{11,1... | collective-permute-start | bytes 350216 | tf_op jit(solution)/shard_map/ppermute | solution.py:20
  (41 other events, 99.5 us)
where the time goes:
time: 387 us; the launch traced here: 381 us
  other arithmetic  174 us (45%)
  local copies, waits for them, and re-layouts  118 us (30%)
  matrix products  40.8 us (11%)
  starting transfers between devices  39 us (10%)
  waiting for transfers between devices  7.08 us (2%)
    add x1, other arithmetic, deposit(): total + padded[1 - move_x:1 - move_x + size_x, 1 - move_y:1 - move_y + si...  139 us
    unnamed x183, local copies, waits for them, and re-layouts  29.6 us
    gather x4, local copies, waits for them, and re-layouts, collide(): bounce = states[opposite] - fluid_eq[opposite] - (states - solid_eq)  14.7 us
    ppermute x4, starting transfers between devices, padded_2(): lax.ppermute(head, axis, [((i + 1) % count, i) for i in range(count)])  13.7 us
    dot_general x2, matrix products, collide(): projected = jnp.dot(to_moments, off_eq, precision=lax.Precision.HIGHEST)  13.5 us
    scatter-add x1, other arithmetic, deposit(): centred = jnp.zeros((cells, 108), jnp.float32).at[target].add(row_values)  13.4 us
    dot_general x3, matrix products, equilibrium(): projected = jnp.dot(lattice_vel, flow, precision=lax.Precision.HIGHEST)  13.3 us
    another operation x7, local copies, waits for them, and re-layouts, stream(): return jnp.stack(read, axis=0)  12.9 us
  transfers between devices with their start and end apart: 16, of which 4 were waited for; matrix products, arithmetic and copies ran while one was open for 22% of the time, Pallas kernels for 0%

commit v1 on v0

v1 whole, which is shorter than its diff:
```python
import functools

import jax
import jax.numpy as jnp
import numpy as np
from jax import lax
from jax.experimental import pallas as pl
from jax.experimental.pallas import tpu as pltpu
from jax.sharding import PartitionSpec as P

CAP = 4
MESH = pl.DeviceIdType.MESH
F32 = jnp.float32
BF16 = jnp.bfloat16
AXIS_PAIRS = ((0, 1), (0, 2), (1, 2))
SIDES = ((-1, -1), (-1, 0), (-1, 1), (0, -1), (0, 1), (1, -1), (1, 0), (1, 1))
PAD = 8


def lattice():
    vectors = [(0, 0, 0)]
    for axis_one in range(3):
        for orient in (1, -1):
            vector_one = [0, 0, 0]
            vector_one[axis_one] = orient
            vectors.append(tuple(vector_one))
    for axis_one, axis_two in AXIS_PAIRS:
        for orient in (1, -1):
            for second in (1, -1):
                vector_one = [0, 0, 0]
                vector_one[axis_one] = orient
                vector_one[axis_two] = second
                vectors.append(tuple(vector_one))
    return vectors


VEL = lattice()
INDEX = {vector: number for number, vector in enumerate(VEL)}
OPP = [INDEX[tuple(-part for part in vector)] for vector in VEL]
PLACES = (
    [number for number in range(19) if VEL[number][0] == 1]
    + [number for number in range(19) if VEL[number][0] == -1]
    + [number for number in range(19) if VEL[number][0] == 0]
)
SLOT = {number: place for place, number in enumerate(PLACES)}
UP = [number for number in range(19) if VEL[number][1] == 1]
DOWN = [number for number in range(19) if VEL[number][1] == -1]


def relaxation_terms():
    speeds = np.array(VEL) * 1.0
    length = (speeds**2).sum(axis=1)
    weights = np.where(length == 0, 1.0 / 3.0, np.where(length == 1, 1.0 / 18.0, 1.0 / 36.0))
    along_x, along_y, along_z = (speeds[:, 0], speeds[:, 1], speeds[:, 2])
    rows_list = [
        np.ones(19),
        along_x,
        along_y,
        along_z,
        length,
        3 * along_x**2 - length,
        along_y**2 - along_z**2,
        along_x * along_y,
        along_y * along_z,
        along_x * along_z,
        along_x * length,
        along_y * length,
        along_z * length,
        along_x * (along_y**2 - along_z**2),
        along_y * (along_z**2 - along_x**2),
        along_z * (along_x**2 - along_y**2),
        length**2,
        (3 * along_x**2 - length) * length,
        (along_y**2 - along_z**2) * length,
    ]
    basis_rows = []
    for candidate in rows_list:
        for earlier in basis_rows:
            candidate = candidate - np.dot(candidate, earlier) * earlier
        basis_rows.append(candidate / np.sqrt(np.dot(candidate, candidate)))
    basis = np.array(basis_rows)

    means = np.zeros((19, 19))
    means[0, 0] = 1.0
    for number, vector in enumerate(VEL):
        used = [axis for axis in range(3) if vector[axis]]
        if len(used) == 1:
            axis = used[0]
            means[1 + axis, number] = 0.5
            means[7 + axis, number] = 0.5 * vector[axis]
        elif len(used) == 2:
            pair = AXIS_PAIRS.index(tuple(used))
            one, two = vector[used[0]], vector[used[1]]
            means[4 + pair, number] = 0.25
            means[10 + 2 * pair, number] = 0.25 * one
            means[11 + 2 * pair, number] = 0.25 * two
            means[16 + pair, number] = 0.25 * one * two
    combine = np.zeros((19, 19))
    entries = [
        {0: 1},
        {1: 1, 2: 1, 3: 1},
        {4: 1, 5: 1, 6: 1},
        {1: 2, 2: -1, 3: -1},
        {4: 1, 5: 1, 6: -2},
        {2: 1, 3: -1},
        {4: 1, 5: -1},
        {7: 1},
        {10: 1, 12: 1},
        {10: 1, 12: -1},
        {8: 1},
        {11: 1, 14: 1},
        {11: 1, 14: -1},
        {9: 1},
        {13: 1, 15: 1},
        {13: 1, 15: -1},
        {16: 1},
        {17: 1},
        {18: 1},
    ]
    for row_number, entry in enumerate(entries):
        for column, factor in entry.items():
            combine[row_number, column] = factor
    scale = np.array(
        [1, 1 / 3, 1 / 3, 1 / 6, 1 / 6, 0.5, 0.5]
        + [1, 0.5, 0.5] * 3
        + [1, 1, 1]
    )
    to_symmetric = combine @ means
    back = np.linalg.inv(to_symmetric)
    terms = {}
    for rate in range(19):
        part = (
            scale[:, None]
            * to_symmetric
            @ np.diag(1.0 / weights)
            @ np.outer(basis[rate], basis[rate])
            @ np.diag(weights)
            @ back
        )
        for row_number in range(19):
            for column in range(19):
                if abs(part[row_number, column]) > 1e-9:
                    terms.setdefault((row_number, column), []).append(
                        (rate, float(part[row_number, column]))
                    )
    return terms


TERMS = relaxation_terms()
ENTRY = {where: number for number, where in enumerate(sorted(TERMS))}


def to_means(value):
    mean = [None] * 19
    mean[0] = value[0]
    for axis in range(3):
        ahead, behind = value[1 + 2 * axis], value[2 + 2 * axis]
        mean[1 + axis] = 0.5 * (ahead + behind)
        mean[7 + axis] = 0.5 * (ahead - behind)
    for pair in range(3):
        pp, pm, mp, mm = value[7 + 4 * pair : 11 + 4 * pair]
        even_one, odd_one = (pp + mm), (pp - mm)
        even_two, odd_two = (pm + mp), (pm - mp)
        mean[4 + pair] = 0.25 * (even_one + even_two)
        mean[16 + pair] = 0.25 * (even_one - even_two)
        mean[10 + 2 * pair] = 0.25 * (odd_one + odd_two)
        mean[11 + 2 * pair] = 0.25 * (odd_one - odd_two)
    return mean


def from_means(mean):
    value = [None] * 19
    value[0] = mean[0]
    for axis in range(3):
        value[1 + 2 * axis] = mean[1 + axis] + mean[7 + axis]
        value[2 + 2 * axis] = mean[1 + axis] - mean[7 + axis]
    for pair in range(3):
        even_one = mean[4 + pair] + mean[16 + pair]
        even_two = mean[4 + pair] - mean[16 + pair]
        odd_one = mean[10 + 2 * pair] + mean[11 + 2 * pair]
        odd_two = mean[10 + 2 * pair] - mean[11 + 2 * pair]
        value[7 + 4 * pair] = even_one + odd_one
        value[8 + 4 * pair] = even_two + odd_two
        value[9 + 4 * pair] = even_two - odd_two
        value[10 + 4 * pair] = even_one - odd_one
    return value


def equilibrium_means(density, impulse, triple):
    half = [0.5 * part for part in triple]
    square = [impulse[axis] * half[axis] for axis in range(3)]
    rest = density - (square[0] + square[1] + square[2]) * (1.0 / 3.0)
    axes = [rest + square[axis] for axis in range(3)]
    mean = [rest] + axes
    mean += [axes[one] + square[two] for one, two in AXIS_PAIRS]
    mean += list(impulse)
    for one, two in AXIS_PAIRS:
        mean += [impulse[one], impulse[two]]
    mean += [impulse[one] * triple[two] for one, two in AXIS_PAIRS]
    return mean


def relax_means(off, coefficient):
    plus = [None] * 19
    plus[0] = off[0]
    pair_sum = off[2] + off[3]
    plus[1] = off[1] + pair_sum
    plus[3] = off[1] + off[1] - pair_sum
    plus[5] = off[2] - off[3]
    pair_sum = off[4] + off[5]
    plus[2] = pair_sum + off[6]
    plus[4] = pair_sum - (off[6] + off[6])
    plus[6] = off[4] - off[5]
    for axis, (one, two) in enumerate(((10, 12), (11, 14), (13, 15))):
        plus[7 + 3 * axis] = off[7 + axis]
        plus[8 + 3 * axis] = off[one] + off[two]
        plus[9 + 3 * axis] = off[one] - off[two]
    plus[16:19] = off[16:19]
    made = []
    for row_number in range(19):
        total = None
        for column in range(19):
            if (row_number, column) in ENTRY:
                term = coefficient(ENTRY[row_number, column]) * plus[column]
                total = term if total is None else total + term
        made.append(total)
    out = [None] * 19
    out[0] = made[0]
    lower = made[1] - made[3]
    out[1] = made[1] + (made[3] + made[3])
    out[2] = lower + made[5]
    out[3] = lower - made[5]
    upper = made[2] + made[4]
    out[4] = upper + made[6]
    out[5] = upper - made[6]
    out[6] = made[2] - (made[4] + made[4])
    for axis, (one, two) in enumerate(((10, 12), (11, 14), (13, 15))):
        out[7 + axis] = made[7 + 3 * axis]
        out[one] = made[8 + 3 * axis] + made[9 + 3 * axis]
        out[two] = made[8 + 3 * axis] - made[9 + 3 * axis]
    out[16:19] = made[16:19]
    return out


def collide(value, solid, solid_triple, coefficient):
    mean = to_means(value)
    ninth, third = 1.0 / 9.0, 1.0 / 3.0
    density = mean[0] * third + (
        (mean[1] + mean[2]) + (mean[3] + mean[4]) + (mean[5] + mean[6])
    ) * ninth
    impulse = [
        (mean[7 + axis] + (mean[one] + mean[two])) * third
        for axis, (one, two) in enumerate(((10, 12), (11, 14), (13, 15)))
    ]
    inverse = 1.0 / density
    triple = [part * inverse for part in impulse]
    fluid = equilibrium_means(density, impulse, triple)
    wall = equilibrium_means(density, [density * part for part in solid_triple], solid_triple)
    off = [mean[number] - fluid[number] for number in range(19)]
    relaxed = relax_means(off, coefficient)
    fluid_part = 1.0 - solid
    post = []
    for number in range(19):
        odd = 7 <= number < 16
        bounced = wall[number] - off[number] if odd else wall[number] + off[number]
        post.append(fluid_part * (mean[number] - relaxed[number]) + solid * bounced)
    return from_means(post)


def main_kernel(
    sizes, rates, velocity, change, fractions, anchor, destination, populations, sent2,
    start, sent1, coef, payload, outbox, inbox, values, spread, across, solids,
    rows_out, rows_in, ends_out, ends_in,
    load_sem, mail_send, mail_recv, halo_send, halo_recv,
):
    size_x, size_y, size_z, table = sizes
    tiles = size_y // 8
    me_x, me_y = lax.axis_index("gx"), lax.axis_index("gy")
    count_x, count_y = lax.axis_size("gx"), lax.axis_size("gy")

    def there(side):
        return side[1] == 0 or (me_y < count_y - 1 if side[1] > 0 else me_y > 0)

    def device(side):
        return (lax.rem(me_x + side[0] + count_x, count_x), me_y + side[1])

    def when_there(side, act):
        if side[1] == 0:
            act()
        else:
            pl.when(there(side))(act)

    load = pltpu.make_async_copy(populations, start, load_sem)
    load.start()
    inbox[...] = jnp.zeros_like(inbox)

    barrier = pltpu.get_barrier_semaphore()
    for side in SIDES:
        def greet(side=side):
            pl.semaphore_signal(barrier, inc=1, device_id=device(side), device_id_type=MESH)
        when_there(side, greet)

    place = anchor[...]
    place_x = lax.shift_right_logical(place, 13)
    place_y = lax.bitwise_and(lax.shift_right_logical(place, 8), 31)
    place_z = lax.bitwise_and(place, 255)
    moved = velocity[...] + change[...]
    payload[...] = jnp.zeros_like(payload)
    payload[0:3, :] = moved
    payload[3:4, :] = place_x.astype(F32)
    payload[4:5, :] = place_y.astype(F32)
    payload[5:6, :] = place_z.astype(F32)
    for plane in range(3):
        payload[8 + 16 * plane : 17 + 16 * plane, :] = fractions[9 * plane : 9 * plane + 9, :]
    code = destination[...]
    row = lax.broadcasted_iota(jnp.int32, (64, table), 0)
    group = lax.shift_right_logical(row, 3)
    wanted = group + jnp.where(group >= 4, 1, 0)
    matches = jnp.broadcast_to(code, (64, table)) == wanted
    chosen = jnp.where(matches, 1.0, 0.0)
    earlier = jnp.where(
        lax.broadcasted_iota(jnp.int32, (table, table), 0)
        <= lax.broadcasted_iota(jnp.int32, (table, table), 1),
        1.0,
        0.0,
    ).astype(BF16)
    ranks = jnp.dot(chosen.astype(BF16), earlier, preferred_element_type=F32)
    rank_of_row = (lax.bitwise_and(row, 7) + 1).astype(F32)
    picked = jnp.where(ranks == rank_of_row, chosen, 0.0).astype(BF16)
    whole = payload[...]
    high = whole.astype(BF16)
    rest = whole - high.astype(F32)
    middle = rest.astype(BF16)
    low = (rest - middle.astype(F32)).astype(BF16)
    contract = (((1,), (1,)), ((), ()))
    packed = lax.dot_general(picked, high, contract, preferred_element_type=F32)
    packed += lax.dot_general(picked, middle, contract, preferred_element_type=F32)
    packed += lax.dot_general(picked, low, contract, preferred_element_type=F32)
    outbox[...] = jnp.zeros_like(outbox)
    for number in range(8):
        outbox[number, :, 0:56] = packed[8 * number : 8 * number + 8, :]

    inside = jnp.logical_and(me_y > 0, me_y < count_y - 1)
    pl.when(inside)(lambda: pl.semaphore_wait(barrier, 8))
    pl.when(jnp.logical_not(inside))(lambda: pl.semaphore_wait(barrier, 5))

    def mail(number):
        return pltpu.make_async_remote_copy(
            src_ref=outbox.at[number],
            dst_ref=inbox.at[number],
            send_sem=mail_send.at[number],
            recv_sem=mail_recv.at[number],
            device_id=device(SIDES[number]),
            device_id_type=MESH,
        )

    for number, side in enumerate(SIDES):
        when_there(side, lambda number=number: mail(number).start())

    for where, number in ENTRY.items():
        total = None
        for rate, factor in TERMS[where]:
            term = rates[rate] * factor
            total = term if total is None else total + term
        coef[number] = jnp.full((8, 128), total, F32)

    def deposit(many, at_x, at_y, at_z, speeds, planes):
        first = at_x == 1.0
        second = at_x == 2.0
        for x in range(size_x):
            near = jnp.where(first, planes[x], 0.0) if x < 3 else jnp.zeros_like(planes[0])
            if x >= 1:
                near = jnp.where(second, planes[x - 1], near)
            for c in range(4):
                part = near if c == 0 else near * speeds[c - 1]
                upper = part.astype(BF16).astype(F32)
                values[0, c, x, 0:9, 0:many] = upper
                values[1, c, x, 0:9, 0:many] = part - upper
        along_y = lax.broadcasted_iota(jnp.int32, (size_y, many), 0).astype(F32)
        ones_y = [
            jnp.where(along_y == at_y + (dy - 1.0), 1.0, 0.0).astype(BF16) for dy in range(3)
        ]
        along_z = lax.broadcasted_iota(jnp.int32, (size_z, many), 0).astype(F32)
        for dz in range(3):
            across[:, dz * many : dz * many + many] = jnp.where(
                along_z == at_z + (dz - 1.0), 1.0, 0.0
            ).astype(BF16)
            for s in range(2):
                for c in range(4):
                    for x in range(size_x):
                        total = None
                        for dy in range(3):
                            line = values[s, c, x, 3 * dy + dz : 3 * dy + dz + 1, 0:many]
                            line = jnp.broadcast_to(line, (size_y, many)).astype(BF16)
                            term = ones_y[dy] * line
                            total = term if total is None else total + term
                        base = ((s * 4 + c) * size_x + x) * size_y
                        spread[base : base + size_y, dz * many : dz * many + many] = total
        both = lax.dot_general(
            spread[:, 0 : 3 * many], across[:, 0 : 3 * many], contract, preferred_element_type=F32
        )
        half = 4 * size_x * size_y
        return both[0:half] + both[half:]

    staying = code == 4
    planes = [
        jnp.where(staying, payload[8 + 16 * plane : 17 + 16 * plane, :], 0.0) for plane in range(3)
    ]
    solids[...] = deposit(
        table,
        payload[3:4, :],
        payload[4:5, :],
        payload[5:6, :],
        [payload[axis : axis + 1, :] for axis in range(3)],
        planes,
    )

    for number, side in enumerate(SIDES):
        back = (-side[0], -side[1])
        when_there(back, lambda number=number: mail(number).wait_recv())
    came = jnp.concatenate([inbox[...].reshape(64, 128), jnp.zeros((64, 128), F32)], axis=0).T
    solids[...] += deposit(
        128,
        came[3:4, :],
        came[4:5, :],
        came[5:6, :],
        [came[axis : axis + 1, :] for axis in range(3)],
        [came[8 + 16 * plane : 17 + 16 * plane, :] for plane in range(3)],
    )

    lane = lax.broadcasted_iota(jnp.int32, (8, 128), 1)
    plane_rows = size_x * size_y

    def rolled(halves, shift):
        turned = [pltpu.roll(half, shift % 128, 1) for half in halves]
        edge = lane == (0 if shift == 1 else 127)
        return [jnp.where(edge, turned[1 - h], turned[h]) for h in range(2)]

    def chunk(step, x, tile):
        posts = []
        for h in range(2):
            at = pl.ds(pl.multiple_of(x * size_y + tile * 8, 8), 8)
            lanes = slice(128 * h, 128 * h + 128)
            whole_rows = [
                pl.ds(pl.multiple_of(c * plane_rows + x * size_y + tile * 8, 8), 8)
                for c in range(4)
            ]
            fields = [solids[whole_rows[c], lanes] for c in range(4)]
            if step == 0:
                value = [
                    start[number, x, pl.ds(pl.multiple_of(tile * 8, 8), 8), lanes]
                    for number in range(19)
                ]
                inverse = 3.0 / (fields[0] + 1e-06)
                solid = jnp.minimum(fields[0], 1.0)
                triple = [fields[1 + axis] * inverse for axis in range(3)]
                solids[whole_rows[0], lanes] = solid
                for axis in range(3):
                    solids[whole_rows[1 + axis], lanes] = triple[axis]
            else:
                value = [
                    sent1[
                        SLOT[number],
                        x + (1 - VEL[number][0]),
                        h,
                        pl.ds(tile * 8 + (PAD - VEL[number][1]), 8),
                        :,
                    ]
                    for number in range(19)
                ]
                solid, triple = fields[0], fields[1:]
            posts.append(collide(value, solid, triple, lambda number: coef[number]))
        out = sent1 if step == 0 else sent2
        rows = pl.ds(pl.multiple_of(tile * 8 + PAD, 8), 8)
        for number in range(19):
            halves = [posts[0][number], posts[1][number]]
            if VEL[number][2]:
                halves = rolled(halves, VEL[number][2])
            for h in range(2):
                out[SLOT[number], x + 1, h, rows, :] = halves[h]

    def sweep(step, places):
        def body(turn, carry):
            chunk(step, *places(turn))
            return carry

        return body

    outer = lambda turn: ((turn // tiles) * (size_x - 1), turn % tiles)
    rims = lambda turn: (1 + turn // 2, (turn % 2) * (tiles - 1))
    inner = lambda turn: (1 + turn // (tiles - 2), 1 + turn % (tiles - 2))

    def side_of(kind, number):
        if kind == "x":
            return ((1, 0), (-1, 0))[number]
        if kind == "y":
            return ((0, 1), (0, -1))[number]
        return ((1, 1), (-1, 1), (1, -1), (-1, -1))[number]

    def halo(step, kind, number):
        out = sent1 if step == 0 else sent2
        side = side_of(kind, number)
        if kind == "x":
            rows = pl.ds(PAD, size_y)
            source = out.at[pl.ds(5 * number, 5), size_x if number == 0 else 1, :, rows, :]
            target = out.at[pl.ds(5 * number, 5), 0 if number == 0 else size_x + 1, :, rows, :]
            sem = number
        elif kind == "y":
            source, target = rows_out.at[step, number], rows_in.at[step, number]
            sem = 2 + number
        else:
            source, target = ends_out.at[step, number], ends_in.at[step, number]
            sem = 4 + number
        return pltpu.make_async_remote_copy(
            src_ref=source,
            dst_ref=target,
            send_sem=halo_send.at[step, sem],
            recv_sem=halo_recv.at[step, sem],
            device_id=device(side),
            device_id_type=MESH,
        )

    HALOS = [("x", 0), ("x", 1), ("y", 0), ("y", 1)] + [("e", number) for number in range(4)]

    def begin(step, kinds):
        for kind, number in HALOS:
            if kind in kinds:
                when_there(
                    side_of(kind, number),
                    lambda kind=kind, number=number: halo(step, kind, number).start(),
                )

    def arrive(step, kinds):
        for kind, number in HALOS:
            if kind in kinds:
                side = side_of(kind, number)
                when_there(
                    (-side[0], -side[1]),
                    lambda kind=kind, number=number: halo(step, kind, number).wait_recv(),
                )

    def stage_rows(step):
        out = sent1 if step == 0 else sent2
        for number, (kinds, row) in enumerate(((UP, PAD + size_y - 1), (DOWN, PAD))):
            for order, one in enumerate(kinds):
                for x in range(size_x):
                    for h in range(2):
                        at = (order * size_x + x) * 2 + h
                        rows_out[step, number, at : at + 1, :] = out[
                            SLOT[one], x + 1, h, row : row + 1, :
                        ]
        for number, (side_x, side_y) in enumerate(((1, 1), (-1, 1), (1, -1), (-1, -1))):
            one = INDEX[side_x, side_y, 0]
            row = PAD + size_y - 1 if side_y == 1 else PAD
            x = size_x if side_x == 1 else 1
            for h in range(2):
                ends_out[step, number, h : h + 1, :] = out[SLOT[one], x, h, row : row + 1, :]

    def fill_rows(step):
        out = sent1 if step == 0 else sent2
        for number, (kinds, sign) in enumerate(((UP, 1), (DOWN, -1))):
            to_row = PAD - 1 if sign == 1 else PAD + size_y
            own_tile = PAD if sign == 1 else PAD + size_y - 8
            own_row = 0 if sign == 1 else 7

            def from_neighbour(number=number, kinds=kinds, to_row=to_row):
                for order, one in enumerate(kinds):
                    for x in range(size_x):
                        for h in range(2):
                            at = (order * size_x + x) * 2 + h
                            out[SLOT[one], x + 1, h, to_row : to_row + 1, :] = rows_in[
                                step, number, at : at + 1, :
                            ]

            def from_wall(kinds=kinds, to_row=to_row, own_tile=own_tile, own_row=own_row):
                for one in kinds:
                    for x in range(size_x):
                        halves = [
                            out[SLOT[OPP[one]], x + 1, h, own_tile : own_tile + 8, :]
                            for h in range(2)
                        ]
                        if VEL[one][2]:
                            halves = rolled(halves, VEL[one][2])
                        for h in range(2):
                            out[SLOT[one], x + 1 - VEL[one][0], h, to_row : to_row + 1, :] = (
                                halves[h][own_row : own_row + 1, :]
                            )

            wall = me_y == 0 if sign == 1 else me_y == count_y - 1
            pl.when(wall)(from_wall)
            pl.when(jnp.logical_not(wall))(from_neighbour)

    def fill_ends(step):
        out = sent1 if step == 0 else sent2
        for number, (side_x, side_y) in enumerate(((1, 1), (-1, 1), (1, -1), (-1, -1))):
            one = INDEX[side_x, side_y, 0]
            to_row = PAD - 1 if side_y == 1 else PAD + size_y
            to_x = 0 if side_x == 1 else size_x + 1

            def copy_in(number=number, one=one, to_row=to_row, to_x=to_x):
                for h in range(2):
                    out[SLOT[one], to_x, h, to_row : to_row + 1, :] = ends_in[
                        step, number, h : h + 1, :
                    ]

            when_there((-side_x, -side_y), copy_in)

    load.wait()
    lax.fori_loop(0, 2 * tiles, sweep(0, outer), 0)
    begin(0, "x")
    lax.fori_loop(0, 4, sweep(0, rims), 0)
    stage_rows(0)
    begin(0, "ye")
    lax.fori_loop(0, 2 * (tiles - 2), sweep(0, inner), 0)
    lax.fori_loop(0, 2 * (tiles - 2), sweep(1, inner), 0)
    arrive(0, "y")
    fill_rows(0)
    lax.fori_loop(0, 4, sweep(1, rims), 0)
    arrive(0, "xe")
    fill_ends(0)
    lax.fori_loop(0, 2 * tiles, sweep(1, outer), 0)
    begin(1, "x")
    stage_rows(1)
    begin(1, "ye")
    arrive(1, "ye")
    fill_rows(1)
    fill_ends(1)
    arrive(1, "x")
    for number, side in enumerate(SIDES):
        when_there(side, lambda number=number: mail(number).wait_send())
    for step in range(2):
        for kind, number in HALOS:
            when_there(
                side_of(kind, number),
                lambda step=step, kind=kind, number=number: halo(step, kind, number).wait_send(),
            )


def last_kernel(sizes, sent, out, stage, sems):
    size_x, size_y, size_z = sizes
    copies = []
    for x in range(size_x):
        for number in range(19):
            for h in range(2):
                low = PAD - VEL[number][1]
                stage[number, x, :, 128 * h : 128 * h + 128] = sent[
                    SLOT[number], x + 1 - VEL[number][0], h, low : low + size_y, :
                ]
        copies.append(pltpu.make_async_copy(stage.at[:, x], out.at[:, x], sems.at[x]))
        copies[-1].start()
    for copy in copies:
        copy.wait()


def local(populations, relax_rates, velocity, velocity_change, fractions, anchor, destination):
    size_x, size_y, size_z = populations.shape[1:]
    table = anchor.shape[0]
    padded = (19, size_x + 2, 2, size_y + 2 * PAD, 128)
    vmem = pl.BlockSpec(memory_space=pltpu.VMEM)
    rows = 5 * size_x * 2
    sent = pl.pallas_call(
        functools.partial(main_kernel, (size_x, size_y, size_z, table)),
        out_shape=pltpu.VMEM(padded, F32),
        in_specs=[pl.BlockSpec(memory_space=pltpu.SMEM)]
        + [vmem] * 5
        + [pl.BlockSpec(memory_space=pl.ANY)],
        out_specs=vmem,
        scratch_shapes=[
            pltpu.VMEM((19, size_x, size_y, size_z), F32),
            pltpu.VMEM(padded, F32),
            pltpu.VMEM((len(ENTRY), 8, 128), F32),
            pltpu.VMEM((56, table), F32),
            pltpu.VMEM((8, 8, 128), F32),
            pltpu.VMEM((8, 8, 128), F32),
            pltpu.VMEM((2, 4, size_x, 16, table), F32),
            pltpu.VMEM((8 * size_x * size_y, 3 * table), BF16),
            pltpu.VMEM((size_z, 3 * table), BF16),
            pltpu.VMEM((4 * size_x * size_y, size_z), F32),
            pltpu.VMEM((2, 2, rows, 128), F32),
            pltpu.VMEM((2, 2, rows, 128), F32),
            pltpu.VMEM((2, 4, 2, 128), F32),
            pltpu.VMEM((2, 4, 2, 128), F32),
            pltpu.SemaphoreType.DMA,
            pltpu.SemaphoreType.DMA((8,)),
            pltpu.SemaphoreType.DMA((8,)),
            pltpu.SemaphoreType.DMA((2, 8)),
            pltpu.SemaphoreType.DMA((2, 8)),
        ],
        compiler_params=pltpu.CompilerParams(
            collective_id=0, has_side_effects=True, vmem_limit_bytes=48 * 1024 * 1024
        ),
    )(
        relax_rates,
        velocity,
        velocity_change,
        fractions,
        anchor.reshape(1, table),
        destination.reshape(1, table),
        populations,
    )
    return pl.pallas_call(
        functools.partial(last_kernel, (size_x, size_y, size_z)),
        out_shape=jax.ShapeDtypeStruct(populations.shape, F32),
        in_specs=[vmem],
        out_specs=pl.BlockSpec(memory_space=pl.ANY),
        scratch_shapes=[
            pltpu.VMEM((19, size_x, size_y, size_z), F32),
            pltpu.SemaphoreType.DMA((size_x,)),
        ],
        compiler_params=pltpu.CompilerParams(vmem_limit_bytes=24 * 1024 * 1024),
    )(sent)


def solution(mesh):
    placed = (
        P(None, "gx", "gy", None),
        P(),
        P(None, ("gx", "gy")),
        P(None, ("gx", "gy")),
        P(None, ("gx", "gy")),
        P(("gx", "gy")),
        P(("gx", "gy")),
    )
    return jax.shard_map(
        local, mesh=mesh, in_specs=placed, out_specs=P(None, "gx", "gy", None), check_vma=False
    )
```

time: 387 us -> 32.7 us (0.08); the launches traced: 381 us -> 32.4 us
  other arithmetic: 174 us -> 0 us
  local copies, waits for them, and re-layouts: 118 us -> 4.25 us
  matrix products: 40.8 us -> 0 us
  starting transfers between devices: 39 us -> 0 us
  Pallas kernels: 0 us -> 28.2 us
  waiting for transfers between devices: 7.08 us -> 0 us
    add x2 -> x0, other arithmetic: 140 us -> none  [the longest x1 139 us: deposit(): total + padded[1 - move_x:1 - move_x + size_x, 1 - move_y:1 - move_y + si...]
    dot_general x8 -> x0, matrix products: 40.8 us -> none  [the longest x2 13.5 us: collide(): projected = jnp.dot(to_moments, off_eq, precision=lax.Precision.HIGHEST)]
    ppermute x16 -> x0, starting transfers between devices: 39 us -> none  [the longest x4 13.7 us: padded_2(): lax.ppermute(head, axis, [((i + 1) % count, i) for i in range(count)])]
    pallas_call x0 -> x2, Pallas kernels: none -> 28.2 us  [the longest x1 26.6 us: local(): pl.pallas_call(functools.partial(main_kernel, (size_x, size_y, size_z, ta...]
    unnamed x183 -> x12, local copies, waits for them, and re-layouts: 29.6 us -> 4.25 us
    squeeze x31 -> x0, local copies, waits for them, and re-layouts: 22.1 us -> none  [the longest x8 11.8 us: stream(): pulled = jnp.where(coord_y == 0, post[opposite[number]], pulled)]
    slice x29 -> x0, local copies, waits for them, and re-layouts: 15 us -> none  [the longest x2 8.52 us: stream(): pulled = jnp.where(coord_y == last_row, post[opposite[number]], pulled)]
    gather x4 -> x0, local copies, waits for them, and re-layouts: 14.7 us -> none  [collide(): bounce = states[opposite] - fluid_eq[opposite] - (states - solid_eq)]
  transfers between devices with their start and end apart: 16 -> 0, of which waited for: 4 -> 0; matrix products, arithmetic and copies ran while one was open for 22% -> 0% of each run, Pallas kernels for 0% -> 0%
where the time goes in v1:
time: 32.7 us; the launch traced here: 32.4 us
  Pallas kernels  28.2 us (86%)
  local copies, waits for them, and re-layouts  4.25 us (13%)
    pallas_call x1, Pallas kernels, local(): pl.pallas_call(functools.partial(main_kernel, (size_x, size_y, size_z, ta...  26.6 us
    unnamed x12, local copies, waits for them, and re-layouts  4.25 us
    pallas_call x1, Pallas kernels, local(): pl.pallas_call(functools.partial(last_kernel, (size_x, size_y, size_z)),...  1.52 us

profile of v1, /device:TPU:0, one launch (start us, length us, event | category | flops | bytes accessed | tf_op | source)
XLA Modules:
  0.0 32.4 jit_solution(3104754338090543306)
XLA Ops:
  0.0 0.0 copy-start
  0.0 0.8 %copy-done = f32[27,512]{1,0:T(8,128)S(1)} copy-done((f32[27,512]{1,0:T(8,128)S(1)}, f32[27,512]{1,0:T(8,128)}, u32[]{:S(2)}) %copy-start) | copy-done | bytes 55320
  0.8 0.0 copy-start.1
  0.8 0.7 %copy-done.1 = f32[3,512]{1,0:T(4,128)S(1)} copy-done((f32[3,512]{1,0:T(4,128)S(1)}, f32[3,512]{1,0:T(4,128)}, u32[]{:S(2)}) %copy-start.1) | copy-done | bytes 6168
  1.5 0.0 copy-start.2
  1.5 0.7 %copy-done.2 = f32[3,512]{1,0:T(4,128)S(1)} copy-done((f32[3,512]{1,0:T(4,128)S(1)}, f32[3,512]{1,0:T(4,128)}, u32[]{:S(2)}) %copy-start.2) | copy-done | bytes 6168
  2.2 0.0 copy-start.3
  2.2 0.7 %copy-done.3 = s32[512]{0:T(512)S(1)} copy-done((s32[512]{0:T(512)S(1)}, s32[512]{0:T(512)}, u32[]{:S(2)}) %copy-start.3) | copy-done | bytes 2072
  2.9 0.0 copy-start.4
  2.9 0.7 %copy-done.4 = s32[512]{0:T(512)S(1)} copy-done((s32[512]{0:T(512)S(1)}, s32[512]{0:T(512)}, u32[]{:S(2)}) %copy-start.4) | copy-done | bytes 2072
  3.6 0.0 copy-start.5
  3.6 0.7 %copy-done.5 = f32[19]{0:T(128)S(1)} copy-done((f32[19]{0:T(128)S(1)}, f32[19]{0:T(128)}, u32[]{:S(2)}) %copy-start.5) | copy-done | bytes 100
  4.3 26.6 %shard_map.73.sent = f32[19,6,2,48,128]{4,3,2,1,0:T(8,128)S(1)} custom-call(f32[19]{0:T(128)S(1)} %copy-done.5, f32[3,512]{1,0:T(4,128)S(1)} %copy-done.1, f32[3,512]{1,0:T(4,128)S(1)} %copy-done.2, f32[27,512]{1,0:T(8,128)S(1)} %copy-done, s32[1,512]{1,0:T(1,128)S(1)} %bitcast.2, s32[1,512]{1,0:T(1,128)S(1)} %bitcast.3, f32[19,4,32,256]{3,2,1,0:T(8,128)} %populations.1), custom_call_target="tpu_custom_call" | custom-call | tf_op jit(solution)/shard_map/pallas_call | solution.py:661
  30.9 1.5 %shard_map.74 = f32[19,4,32,256]{3,2,1,0:T(8,128)} custom-call(f32[19,6,2,48,128]{4,3,2,1,0:T(8,128)S(1)} %shard_map.73.sent), custom_call_target="tpu_custom_call" | custom-call | tf_op jit(solution)/shard_map/pallas_call | solution.py:701
Async XLA Ops:
  0.0 0.8 %copy-start = (f32[27,512]{1,0:T(8,128)S(1)}, f32[27,512]{1,0:T(8,128)}, u32[]{:S(2)}) copy-start(f32[27,512]{1,0:T(8,128)} %fractions.1) | copy-start | bytes 165892
  0.8 0.7 %copy-start.1 = (f32[3,512]{1,0:T(4,128)S(1)}, f32[3,512]{1,0:T(4,128)}, u32[]{:S(2)}) copy-start(f32[3,512]{1,0:T(4,128)} %velocity.1) | copy-start | bytes 18436
  1.5 0.7 %copy-start.2 = (f32[3,512]{1,0:T(4,128)S(1)}, f32[3,512]{1,0:T(4,128)}, u32[]{:S(2)}) copy-start(f32[3,512]{1,0:T(4,128)} %change.1) | copy-start | bytes 18436
  2.2 0.7 %copy-start.3 = (s32[512]{0:T(512)S(1)}, s32[512]{0:T(512)}, u32[]{:S(2)}) copy-start(s32[512]{0:T(512)} %param.12) | copy-start | bytes 6148
  2.9 0.7 %copy-start.4 = (s32[512]{0:T(512)S(1)}, s32[512]{0:T(512)}, u32[]{:S(2)}) copy-start(s32[512]{0:T(512)} %param.13) | copy-start | bytes 6148
  3.6 0.7 %copy-start.5 = (f32[19]{0:T(128)S(1)}, f32[19]{0:T(128)}, u32[]{:S(2)}) copy-start(f32[19]{0:T(128)} %rates.1) | copy-start | bytes 232

commit v2 on v1

--- a/solution.py
+++ b/solution.py
@@ -268,10 +268,12 @@
 
 
 def main_kernel(
-    sizes, rates, velocity, change, fractions, anchor, destination, populations, sent2,
-    start, sent1, coef, payload, outbox, inbox, values, spread, across, solids,
+    sizes, rates_hbm, velocity_hbm, change_hbm, fractions_hbm, anchor_hbm, destination_hbm,
+    populations, result,
+    rates, velocity, change, fractions, anchor, destination,
+    start, sent1, sent2, coef, payload, outbox, inbox, values, spread, across, solids,
     rows_out, rows_in, ends_out, ends_in,
-    load_sem, mail_send, mail_recv, halo_send, halo_recv,
+    fetch_sem, load_sem, mail_send, mail_recv, halo_send, halo_recv,
 ):
     size_x, size_y, size_z, table = sizes
     tiles = size_y // 8
@@ -290,6 +292,21 @@
         else:
             pl.when(there(side))(act)
 
+    fetches = [
+        pltpu.make_async_copy(source, target, fetch_sem.at[number])
+        for number, (source, target) in enumerate(
+            (
+                (destination_hbm, destination),
+                (anchor_hbm, anchor),
+                (velocity_hbm, velocity),
+                (change_hbm, change),
+                (fractions_hbm, fractions),
+                (rates_hbm, rates),
+            )
+        )
+    ]
+    for fetch in fetches:
+        fetch.start()
     load = pltpu.make_async_copy(populations, start, load_sem)
     load.start()
     inbox[...] = jnp.zeros_like(inbox)
@@ -300,12 +317,15 @@
             pl.semaphore_signal(barrier, inc=1, device_id=device(side), device_id_type=MESH)
         when_there(side, greet)
 
+    payload[...] = jnp.zeros_like(payload)
+    outbox[...] = jnp.zeros_like(outbox)
+    for fetch in fetches:
+        fetch.wait()
     place = anchor[...]
     place_x = lax.shift_right_logical(place, 13)
     place_y = lax.bitwise_and(lax.shift_right_logical(place, 8), 31)
     place_z = lax.bitwise_and(place, 255)
     moved = velocity[...] + change[...]
-    payload[...] = jnp.zeros_like(payload)
     payload[0:3, :] = moved
     payload[3:4, :] = place_x.astype(F32)
     payload[4:5, :] = place_y.astype(F32)
@@ -336,7 +356,6 @@
     packed = lax.dot_general(picked, high, contract, preferred_element_type=F32)
     packed += lax.dot_general(picked, middle, contract, preferred_element_type=F32)
     packed += lax.dot_general(picked, low, contract, preferred_element_type=F32)
-    outbox[...] = jnp.zeros_like(outbox)
     for number in range(8):
         outbox[number, :, 0:56] = packed[8 * number : 8 * number + 8, :]
 
@@ -486,7 +505,6 @@
 
         return body
 
-    outer = lambda turn: ((turn // tiles) * (size_x - 1), turn % tiles)
     rims = lambda turn: (1 + turn // 2, (turn % 2) * (tiles - 1))
     inner = lambda turn: (1 + turn // (tiles - 2), 1 + turn % (tiles - 2))
 
@@ -497,20 +515,20 @@
             return ((0, 1), (0, -1))[number]
         return ((1, 1), (-1, 1), (1, -1), (-1, -1))[number]
 
-    def halo(step, kind, number):
+    def halo(step, kind, number, piece=0):
         out = sent1 if step == 0 else sent2
         side = side_of(kind, number)
         if kind == "x":
-            rows = pl.ds(PAD, size_y)
+            rows = pl.ds(pl.multiple_of(PAD + 8 * piece, 8), 8)
             source = out.at[pl.ds(5 * number, 5), size_x if number == 0 else 1, :, rows, :]
             target = out.at[pl.ds(5 * number, 5), 0 if number == 0 else size_x + 1, :, rows, :]
-            sem = number
+            sem = 6 + number * tiles + piece
         elif kind == "y":
             source, target = rows_out.at[step, number], rows_in.at[step, number]
-            sem = 2 + number
+            sem = number
         else:
             source, target = ends_out.at[step, number], ends_in.at[step, number]
-            sem = 4 + number
+            sem = 2 + number
         return pltpu.make_async_remote_copy(
             src_ref=source,
             dst_ref=target,
@@ -520,24 +538,30 @@
             device_id_type=MESH,
         )
 
-    HALOS = [("x", 0), ("x", 1), ("y", 0), ("y", 1)] + [("e", number) for number in range(4)]
-
-    def begin(step, kinds):
+    HALOS = [("y", 0), ("y", 1)] + [("e", number) for number in range(4)]
+
+    def begin(step):
         for kind, number in HALOS:
-            if kind in kinds:
-                when_there(
-                    side_of(kind, number),
-                    lambda kind=kind, number=number: halo(step, kind, number).start(),
-                )
-
-    def arrive(step, kinds):
+            when_there(
+                side_of(kind, number),
+                lambda kind=kind, number=number: halo(step, kind, number).start(),
+            )
+
+    def arrive(step):
         for kind, number in HALOS:
-            if kind in kinds:
-                side = side_of(kind, number)
-                when_there(
-                    (-side[0], -side[1]),
-                    lambda kind=kind, number=number: halo(step, kind, number).wait_recv(),
-                )
+            side = side_of(kind, number)
+            when_there(
+                (-side[0], -side[1]),
+                lambda kind=kind, number=number: halo(step, kind, number).wait_recv(),
+            )
+
+    def face_begin(step, piece):
+        for number in range(2):
+            halo(step, "x", number, piece).start()
+
+    def face_arrive(step, piece):
+        for number in range(2):
+            halo(step, "x", number, piece).wait_recv()
 
     def stage_rows(step):
         out = sent1 if step == 0 else sent2
@@ -605,27 +629,72 @@
 
             when_there((-side_x, -side_y), copy_in)
 
+    def final(number, x, tiles_of):
+        for h in range(2):
+            for tile in tiles_of:
+                result[number, x, 8 * tile : 8 * tile + 8, 128 * h : 128 * h + 128] = sent2[
+                    SLOT[number],
+                    x + 1 - VEL[number][0],
+                    h,
+                    8 * tile + PAD - VEL[number][1] : 8 * tile + PAD - VEL[number][1] + 8,
+                    :,
+                ]
+
+    def finish(early):
+        for number in range(19):
+            for x in range(size_x):
+                from_x = 0 <= x - VEL[number][0] < size_x
+                ready = [
+                    tile
+                    for tile in range(tiles)
+                    if from_x
+                    and not (VEL[number][1] == 1 and tile == 0)
+                    and not (VEL[number][1] == -1 and tile == tiles - 1)
+                ]
+                final(number, x, ready if early else [t for t in range(tiles) if t not in ready])
+
+    def edges(step, tile):
+        chunk(step, size_x - 1, tile)
+        chunk(step, 0, tile)
+        face_begin(step, tile)
+
     load.wait()
-    lax.fori_loop(0, 2 * tiles, sweep(0, outer), 0)
-    begin(0, "x")
+
+    @pl.loop(0, tiles)
+    def _(turn):
+        edges(0, turn)
+
     lax.fori_loop(0, 4, sweep(0, rims), 0)
     stage_rows(0)
-    begin(0, "ye")
+    begin(0)
     lax.fori_loop(0, 2 * (tiles - 2), sweep(0, inner), 0)
     lax.fori_loop(0, 2 * (tiles - 2), sweep(1, inner), 0)
-    arrive(0, "y")
+    face_arrive(0, 0)
+    face_arrive(0, 1)
+
+    @pl.loop(1, tiles - 1)
+    def _(turn):
+        face_arrive(0, turn + 1)
+        edges(1, turn)
+
+    arrive(0)
     fill_rows(0)
+    fill_ends(0)
+
+    @pl.loop(0, 2)
+    def _(turn):
+        edges(1, turn * (tiles - 1))
+
     lax.fori_loop(0, 4, sweep(1, rims), 0)
-    arrive(0, "xe")
-    fill_ends(0)
-    lax.fori_loop(0, 2 * tiles, sweep(1, outer), 0)
-    begin(1, "x")
     stage_rows(1)
-    begin(1, "ye")
-    arrive(1, "ye")
+    begin(1)
+    finish(True)
+    for piece in range(tiles):
+        face_arrive(1, piece)
+    arrive(1)
     fill_rows(1)
     fill_ends(1)
-    arrive(1, "x")
+    finish(False)
     for number, side in enumerate(SIDES):
         when_there(side, lambda number=number: mail(number).wait_send())
     for step in range(2):
@@ -634,39 +703,32 @@
                 side_of(kind, number),
                 lambda step=step, kind=kind, number=number: halo(step, kind, number).wait_send(),
             )
-
-
-def last_kernel(sizes, sent, out, stage, sems):
-    size_x, size_y, size_z = sizes
-    copies = []
-    for x in range(size_x):
-        for number in range(19):
-            for h in range(2):
-                low = PAD - VEL[number][1]
-                stage[number, x, :, 128 * h : 128 * h + 128] = sent[
-                    SLOT[number], x + 1 - VEL[number][0], h, low : low + size_y, :
-                ]
-        copies.append(pltpu.make_async_copy(stage.at[:, x], out.at[:, x], sems.at[x]))
-        copies[-1].start()
-    for copy in copies:
-        copy.wait()
+        for number in range(2):
+            for piece in range(tiles):
+                halo(step, "x", number, piece).wait_send()
 
 
 def local(populations, relax_rates, velocity, velocity_change, fractions, anchor, destination):
     size_x, size_y, size_z = populations.shape[1:]
     table = anchor.shape[0]
     padded = (19, size_x + 2, 2, size_y + 2 * PAD, 128)
-    vmem = pl.BlockSpec(memory_space=pltpu.VMEM)
+    hbm = pl.BlockSpec(memory_space=pltpu.HBM)
     rows = 5 * size_x * 2
-    sent = pl.pallas_call(
+    halos = 6 + 2 * (size_y // 8)
+    return pl.pallas_call(
         functools.partial(main_kernel, (size_x, size_y, size_z, table)),
-        out_shape=pltpu.VMEM(padded, F32),
-        in_specs=[pl.BlockSpec(memory_space=pltpu.SMEM)]
-        + [vmem] * 5
-        + [pl.BlockSpec(memory_space=pl.ANY)],
-        out_specs=vmem,
+        out_shape=pltpu.VMEM(populations.shape, F32),
+        in_specs=[hbm] * 7,
+        out_specs=pl.BlockSpec(memory_space=pltpu.VMEM),
         scratch_shapes=[
+            pltpu.SMEM((19,), F32),
+            pltpu.VMEM((3, table), F32),
+            pltpu.VMEM((3, table), F32),
+            pltpu.VMEM((27, table), F32),
+            pltpu.VMEM((1, table), jnp.int32),
+            pltpu.VMEM((1, table), jnp.int32),
             pltpu.VMEM((19, size_x, size_y, size_z), F32),
+            pltpu.VMEM(padded, F32),
             pltpu.VMEM(padded, F32),
             pltpu.VMEM((len(ENTRY), 8, 128), F32),
             pltpu.VMEM((56, table), F32),
@@ -680,35 +742,30 @@
             pltpu.VMEM((2, 2, rows, 128), F32),
             pltpu.VMEM((2, 4, 2, 128), F32),
             pltpu.VMEM((2, 4, 2, 128), F32),
+            pltpu.SemaphoreType.DMA((6,)),
             pltpu.SemaphoreType.DMA,
             pltpu.SemaphoreType.DMA((8,)),
             pltpu.SemaphoreType.DMA((8,)),
-            pltpu.SemaphoreType.DMA((2, 8)),
-            pltpu.SemaphoreType.DMA((2, 8)),
+            pltpu.SemaphoreType.DMA((2, halos)),
+            pltpu.SemaphoreType.DMA((2, halos)),
         ],
         compiler_params=pltpu.CompilerParams(
             collective_id=0, has_side_effects=True, vmem_limit_bytes=48 * 1024 * 1024
         ),
     )(
-        relax_rates,
-        velocity,
-        velocity_change,
-        fractions,
-        anchor.reshape(1, table),
-        destination.reshape(1, table),
-        populations,
+        *(
+            pltpu.with_memory_space_constraint(operand, pltpu.HBM)
+            for operand in (
+                relax_rates,
+                velocity,
+                velocity_change,
+                fractions,
+                anchor.reshape(1, table),
+                destination.reshape(1, table),
+                populations,
+            )
+        )
     )
-    return pl.pallas_call(
-        functools.partial(last_kernel, (size_x, size_y, size_z)),
-        out_shape=jax.ShapeDtypeStruct(populations.shape, F32),
-        in_specs=[vmem],
-        out_specs=pl.BlockSpec(memory_space=pl.ANY),
-        scratch_shapes=[
-            pltpu.VMEM((19, size_x, size_y, size_z), F32),
-            pltpu.SemaphoreType.DMA((size_x,)),
-        ],
-        compiler_params=pltpu.CompilerParams(vmem_limit_bytes=24 * 1024 * 1024),
-    )(sent)
 
 
 def solution(mesh):

time: 32.7 us -> 26.4 us (0.81)
  the two profiles are of different devices: /device:TPU:0 before, /device:TPU:1 now
where the time goes in v2:
time: 26.4 us; the launch traced here: 26.3 us
  Pallas kernels  24.8 us (94%)
  local copies, waits for them, and re-layouts  1.45 us (5%)
    pallas_call x1, Pallas kernels, local(): pl.pallas_call(functools.partial(main_kernel, (size_x, size_y, size_z, ta...  24.8 us
    unnamed x1, local copies, waits for them, and re-layouts  1.45 us

profile of v2, /device:TPU:1, one launch (start us, length us, event | category | flops | bytes accessed | tf_op | source)
XLA Modules:
  0.0 26.3 jit_solution(5331345157088236004)
XLA Ops:
  0.0 24.8 %shard_map.73 = f32[19,4,32,256]{3,2,1,0:T(8,128)S(1)} custom-call(f32[19]{0:T(128)} %rates_hbm.1, f32[3,512]{1,0:T(4,128)} %velocity_hbm.1, f32[3,512]{1,0:T(4,128)} %change_hbm.1, f32[27,512]{1,0:T(8,128)} %fractions_hbm.1, s32[1,512]{1,0:T(1,128)} %bitcast.2, s32[1,512]{1,0:T(1,128)} %bitcast.3, f32[19,4,32,256]{3,2,1,0:T(8,128)} %populations.1), custom_call_target="tpu_custom_call" | custom-call | tf_op jit(solution)/shard_map/pallas_call | solution.py:718
  24.8 1.5 %copy.9 = f32[19,4,32,256]{3,2,1,0:T(8,128)} copy(f32[19,4,32,256]{3,2,1,0:T(8,128)S(1)} %shard_map.73) | data formatting | bytes 4980736

commit v3 on v2

--- a/solution.py
+++ b/solution.py
@@ -242,7 +242,7 @@
     return out
 
 
-def collide(value, solid, solid_triple, coefficient):
+def fluid_part(value, coefficient):
     mean = to_means(value)
     ninth, third = 1.0 / 9.0, 1.0 / 3.0
     density = mean[0] * third + (
@@ -255,15 +255,19 @@
     inverse = 1.0 / density
     triple = [part * inverse for part in impulse]
     fluid = equilibrium_means(density, impulse, triple)
-    wall = equilibrium_means(density, [density * part for part in solid_triple], solid_triple)
     off = [mean[number] - fluid[number] for number in range(19)]
     relaxed = relax_means(off, coefficient)
-    fluid_part = 1.0 - solid
+    return density, [mean[number] - relaxed[number] for number in range(19)], off
+
+
+def solid_part(density, kept, off, solid, solid_triple):
+    wall = equilibrium_means(density, [density * part for part in solid_triple], solid_triple)
+    share = 1.0 - solid
     post = []
     for number in range(19):
         odd = 7 <= number < 16
         bounced = wall[number] - off[number] if odd else wall[number] + off[number]
-        post.append(fluid_part * (mean[number] - relaxed[number]) + solid * bounced)
+        post.append(share * kept[number] + solid * bounced)
     return from_means(post)
 
 
@@ -271,7 +275,7 @@
     sizes, rates_hbm, velocity_hbm, change_hbm, fractions_hbm, anchor_hbm, destination_hbm,
     populations, result,
     rates, velocity, change, fractions, anchor, destination,
-    start, sent1, sent2, coef, payload, outbox, inbox, values, spread, across, solids,
+    start, ahead, sent1, sent2, coef, payload, outbox, inbox, values, spread, across, solids,
     rows_out, rows_in, ends_out, ends_in,
     fetch_sem, load_sem, mail_send, mail_recv, halo_send, halo_recv,
 ):
@@ -291,6 +295,16 @@
             act()
         else:
             pl.when(there(side))(act)
+
+    inbox[...] = jnp.zeros_like(inbox)
+    barrier = pltpu.get_barrier_semaphore()
+    def far(side):
+        return -2 * abs(side[0]) - abs(side[1])
+
+    for side in sorted(SIDES, key=far):
+        def greet(side=side):
+            pl.semaphore_signal(barrier, inc=1, device_id=device(side), device_id_type=MESH)
+        when_there(side, greet)
 
     fetches = [
         pltpu.make_async_copy(source, target, fetch_sem.at[number])
@@ -309,13 +323,6 @@
         fetch.start()
     load = pltpu.make_async_copy(populations, start, load_sem)
     load.start()
-    inbox[...] = jnp.zeros_like(inbox)
-
-    barrier = pltpu.get_barrier_semaphore()
-    for side in SIDES:
-        def greet(side=side):
-            pl.semaphore_signal(barrier, inc=1, device_id=device(side), device_id_type=MESH)
-        when_there(side, greet)
 
     payload[...] = jnp.zeros_like(payload)
     outbox[...] = jnp.zeros_like(outbox)
@@ -373,8 +380,8 @@
             device_id_type=MESH,
         )
 
-    for number, side in enumerate(SIDES):
-        when_there(side, lambda number=number: mail(number).start())
+    for number in sorted(range(8), key=lambda number: far(SIDES[number])):
+        when_there(SIDES[number], lambda number=number: mail(number).start())
 
     for where, number in ENTRY.items():
         total = None
@@ -383,7 +390,8 @@
             total = term if total is None else total + term
         coef[number] = jnp.full((8, 128), total, F32)
 
-    def deposit(many, at_x, at_y, at_z, speeds, planes):
+    def deposit(many, at_x, at_y, at_z, speeds, planes, twice):
+        left = lax.broadcasted_iota(jnp.int32, (1, many), 1) < many // 2
         first = at_x == 1.0
         second = at_x == 2.0
         for x in range(size_x):
@@ -393,8 +401,11 @@
             for c in range(4):
                 part = near if c == 0 else near * speeds[c - 1]
                 upper = part.astype(BF16).astype(F32)
-                values[0, c, x, 0:9, 0:many] = upper
-                values[1, c, x, 0:9, 0:many] = part - upper
+                if twice:
+                    values[0, c, x, 0:9, 0:many] = jnp.where(left, upper, part - upper)
+                else:
+                    values[0, c, x, 0:9, 0:many] = upper
+                    values[1, c, x, 0:9, 0:many] = part - upper
         along_y = lax.broadcasted_iota(jnp.int32, (size_y, many), 0).astype(F32)
         ones_y = [
             jnp.where(along_y == at_y + (dy - 1.0), 1.0, 0.0).astype(BF16) for dy in range(3)
@@ -404,7 +415,7 @@
             across[:, dz * many : dz * many + many] = jnp.where(
                 along_z == at_z + (dz - 1.0), 1.0, 0.0
             ).astype(BF16)
-            for s in range(2):
+            for s in range(1 if twice else 2):
                 for c in range(4):
                     for x in range(size_x):
                         total = None
@@ -415,11 +426,14 @@
                             total = term if total is None else total + term
                         base = ((s * 4 + c) * size_x + x) * size_y
                         spread[base : base + size_y, dz * many : dz * many + many] = total
+        half = 4 * size_x * size_y
         both = lax.dot_general(
-            spread[:, 0 : 3 * many], across[:, 0 : 3 * many], contract, preferred_element_type=F32
+            spread[0 : half if twice else 2 * half, 0 : 3 * many],
+            across[:, 0 : 3 * many],
+            contract,
+            preferred_element_type=F32,
         )
-        half = 4 * size_x * size_y
-        return both[0:half] + both[half:]
+        return both if twice else both[0:half] + both[half:]
 
     staying = code == 4
     planes = [
@@ -432,12 +446,30 @@
         payload[5:6, :],
         [payload[axis : axis + 1, :] for axis in range(3)],
         planes,
+        False,
     )
+
+    load.wait()
+
+    @pl.loop(0, size_x * tiles)
+    def _(turn):
+        x, tile = turn // tiles, turn % tiles
+        rows = pl.ds(pl.multiple_of(tile * 8, 8), 8)
+        for h in range(2):
+            lanes = slice(128 * h, 128 * h + 128)
+            density, kept, off = fluid_part(
+                [start[number, x, rows, lanes] for number in range(19)], lambda number: coef[number]
+            )
+            ahead[38, x, h, rows, :] = density
+            for number in range(19):
+                ahead[number, x, h, rows, :] = kept[number]
+                ahead[19 + number, x, h, rows, :] = off[number]
 
     for number, side in enumerate(SIDES):
         back = (-side[0], -side[1])
         when_there(back, lambda number=number: mail(number).wait_recv())
-    came = jnp.concatenate([inbox[...].reshape(64, 128), jnp.zeros((64, 128), F32)], axis=0).T
+    letters = inbox[...].reshape(64, 128)
+    came = jnp.concatenate([letters, letters], axis=0).T
     solids[...] += deposit(
         128,
         came[3:4, :],
@@ -445,6 +477,7 @@
         came[5:6, :],
         [came[axis : axis + 1, :] for axis in range(3)],
         [came[8 + 16 * plane : 17 + 16 * plane, :] for plane in range(3)],
+        True,
     )
 
     lane = lax.broadcasted_iota(jnp.int32, (8, 128), 1)
@@ -458,7 +491,6 @@
     def chunk(step, x, tile):
         posts = []
         for h in range(2):
-            at = pl.ds(pl.multiple_of(x * size_y + tile * 8, 8), 8)
             lanes = slice(128 * h, 128 * h + 128)
             whole_rows = [
                 pl.ds(pl.multiple_of(c * plane_rows + x * size_y + tile * 8, 8), 8)
@@ -466,10 +498,9 @@
             ]
             fields = [solids[whole_rows[c], lanes] for c in range(4)]
             if step == 0:
-                value = [
-                    start[number, x, pl.ds(pl.multiple_of(tile * 8, 8), 8), lanes]
-                    for number in range(19)
-                ]
+                own = pl.ds(pl.multiple_of(tile * 8, 8), 8)
+                parts = [ahead[number, x, h, own, :] for number in range(39)]
+                density, kept, off = parts[38], parts[0:19], parts[19:38]
                 inverse = 3.0 / (fields[0] + 1e-06)
                 solid = jnp.minimum(fields[0], 1.0)
                 triple = [fields[1 + axis] * inverse for axis in range(3)]
@@ -488,7 +519,8 @@
                     for number in range(19)
                 ]
                 solid, triple = fields[0], fields[1:]
-            posts.append(collide(value, solid, triple, lambda number: coef[number]))
+                density, kept, off = fluid_part(value, lambda number: coef[number])
+            posts.append(solid_part(density, kept, off, solid, triple))
         out = sent1 if step == 0 else sent2
         rows = pl.ds(pl.multiple_of(tile * 8 + PAD, 8), 8)
         for number in range(19):
@@ -538,17 +570,19 @@
             device_id_type=MESH,
         )
 
-    HALOS = [("y", 0), ("y", 1)] + [("e", number) for number in range(4)]
-
-    def begin(step):
-        for kind, number in HALOS:
+    ROWS = [("y", 0), ("y", 1)]
+    ENDS = [("e", number) for number in range(4)]
+    ENDS_UP, ENDS_DOWN = ENDS[:2], ENDS[2:]
+
+    def begin(step, halos):
+        for kind, number in halos:
             when_there(
                 side_of(kind, number),
                 lambda kind=kind, number=number: halo(step, kind, number).start(),
             )
 
-    def arrive(step):
-        for kind, number in HALOS:
+    def arrive(step, halos):
+        for kind, number in halos:
             side = side_of(kind, number)
             when_there(
                 (-side[0], -side[1]),
@@ -573,7 +607,11 @@
                         rows_out[step, number, at : at + 1, :] = out[
                             SLOT[one], x + 1, h, row : row + 1, :
                         ]
-        for number, (side_x, side_y) in enumerate(((1, 1), (-1, 1), (1, -1), (-1, -1))):
+
+    def stage_ends(step, halos):
+        out = sent1 if step == 0 else sent2
+        for kind, number in halos:
+            side_x, side_y = side_of(kind, number)
             one = INDEX[side_x, side_y, 0]
             row = PAD + size_y - 1 if side_y == 1 else PAD
             x = size_x if side_x == 1 else 1
@@ -653,52 +691,55 @@
                 ]
                 final(number, x, ready if early else [t for t in range(tiles) if t not in ready])
 
-    def edges(step, tile):
+    def edges(step, tile, halos=()):
         chunk(step, size_x - 1, tile)
         chunk(step, 0, tile)
+        stage_ends(step, halos)
+        begin(step, halos)
         face_begin(step, tile)
 
-    load.wait()
-
-    @pl.loop(0, tiles)
+    edges(0, 0, ENDS_DOWN)
+    edges(0, tiles - 1, ENDS_UP)
+
+    @pl.loop(1, tiles - 1)
     def _(turn):
         edges(0, turn)
 
     lax.fori_loop(0, 4, sweep(0, rims), 0)
     stage_rows(0)
-    begin(0)
+    begin(0, ROWS)
     lax.fori_loop(0, 2 * (tiles - 2), sweep(0, inner), 0)
     lax.fori_loop(0, 2 * (tiles - 2), sweep(1, inner), 0)
+    arrive(0, ROWS)
+    fill_rows(0)
+    lax.fori_loop(0, 4, sweep(1, rims), 0)
+    arrive(0, ENDS)
+    fill_ends(0)
     face_arrive(0, 0)
     face_arrive(0, 1)
+    edges(1, 0, ENDS_DOWN)
+    for piece in range(2, tiles):
+        face_arrive(0, piece)
+    edges(1, tiles - 1, ENDS_UP)
+    stage_rows(1)
+    begin(1, ROWS)
 
     @pl.loop(1, tiles - 1)
     def _(turn):
-        face_arrive(0, turn + 1)
         edges(1, turn)
 
-    arrive(0)
-    fill_rows(0)
-    fill_ends(0)
-
-    @pl.loop(0, 2)
-    def _(turn):
-        edges(1, turn * (tiles - 1))
-
-    lax.fori_loop(0, 4, sweep(1, rims), 0)
-    stage_rows(1)
-    begin(1)
     finish(True)
+    arrive(1, ROWS)
+    fill_rows(1)
     for piece in range(tiles):
         face_arrive(1, piece)
-    arrive(1)
-    fill_rows(1)
+    arrive(1, ENDS)
     fill_ends(1)
     finish(False)
     for number, side in enumerate(SIDES):
         when_there(side, lambda number=number: mail(number).wait_send())
     for step in range(2):
-        for kind, number in HALOS:
+        for kind, number in ROWS + ENDS:
             when_there(
                 side_of(kind, number),
                 lambda step=step, kind=kind, number=number: halo(step, kind, number).wait_send(),
@@ -728,6 +769,7 @@
             pltpu.VMEM((1, table), jnp.int32),
             pltpu.VMEM((1, table), jnp.int32),
             pltpu.VMEM((19, size_x, size_y, size_z), F32),
+            pltpu.VMEM((39, size_x, 2, size_y, 128), F32),
             pltpu.VMEM(padded, F32),
             pltpu.VMEM(padded, F32),
             pltpu.VMEM((len(ENTRY), 8, 128), F32),

time: 26.4 us -> 25 us (0.947)
  the two profiles are of different devices: /device:TPU:1 before, /device:TPU:0 now
where the time goes in v3:
time: 25 us; the launch traced here: 24.9 us
  Pallas kernels  23.5 us (94%)
  local copies, waits for them, and re-layouts  1.45 us (6%)
    pallas_call x1, Pallas kernels, local(): pl.pallas_call(functools.partial(main_kernel, (size_x, size_y, size_z, ta...  23.5 us
    unnamed x1, local copies, waits for them, and re-layouts  1.45 us

profile of v3, /device:TPU:0, one launch (start us, length us, event | category | flops | bytes accessed | tf_op | source)
XLA Modules:
  0.0 24.9 jit_solution(17933792593537364917)
XLA Ops:
  0.0 23.5 %shard_map.73 = f32[19,4,32,256]{3,2,1,0:T(8,128)S(1)} custom-call(f32[19]{0:T(128)} %rates_hbm.1, f32[3,512]{1,0:T(4,128)} %velocity_hbm.1, f32[3,512]{1,0:T(4,128)} %change_hbm.1, f32[27,512]{1,0:T(8,128)} %fractions_hbm.1, s32[1,512]{1,0:T(1,128)} %bitcast.2, s32[1,512]{1,0:T(1,128)} %bitcast.3, f32[19,4,32,256]{3,2,1,0:T(8,128)} %populations.1), custom_call_target="tpu_custom_call" | custom-call | tf_op jit(solution)/shard_map/pallas_call | solution.py:759
  23.5 1.5 %copy.9 = f32[19,4,32,256]{3,2,1,0:T(8,128)} copy(f32[19,4,32,256]{3,2,1,0:T(8,128)S(1)} %shard_map.73) | data formatting | bytes 4980736

commit v4 on v3

--- a/solution.py
+++ b/solution.py
@@ -390,11 +390,31 @@
             total = term if total is None else total + term
         coef[number] = jnp.full((8, 128), total, F32)
 
-    def deposit(many, at_x, at_y, at_z, speeds, planes, twice):
+    ENDMOST, MIDDLE = (0, size_x - 1), tuple(range(1, size_x - 1))
+    turned = {x: number for number, x in enumerate(ENDMOST + MIDDLE)}
+    block = 4 * size_y
+
+    def rows_of(x, c, tile):
+        number = turned[x] if isinstance(x, int) else x + 1
+        return pl.ds(pl.multiple_of(number * block + c * size_y + tile * 8, 8), 8)
+
+    def prepare(many, at_y, at_z):
+        along_y = lax.broadcasted_iota(jnp.int32, (size_y, many), 0).astype(F32)
+        along_z = lax.broadcasted_iota(jnp.int32, (size_z, many), 0).astype(F32)
+        for dz in range(3):
+            across[:, dz * many : dz * many + many] = jnp.where(
+                along_z == at_z + (dz - 1.0), 1.0, 0.0
+            ).astype(BF16)
+        return [
+            jnp.where(along_y == at_y + (dy - 1.0), 1.0, 0.0).astype(BF16) for dy in range(3)
+        ]
+
+    def deposit(many, at_x, ones_y, speeds, planes, twice, xs):
         left = lax.broadcasted_iota(jnp.int32, (1, many), 1) < many // 2
         first = at_x == 1.0
         second = at_x == 2.0
-        for x in range(size_x):
+        half = len(xs) * block
+        for x in xs:
             near = jnp.where(first, planes[x], 0.0) if x < 3 else jnp.zeros_like(planes[0])
             if x >= 1:
                 near = jnp.where(second, planes[x - 1], near)
@@ -406,27 +426,18 @@
                 else:
                     values[0, c, x, 0:9, 0:many] = upper
                     values[1, c, x, 0:9, 0:many] = part - upper
-        along_y = lax.broadcasted_iota(jnp.int32, (size_y, many), 0).astype(F32)
-        ones_y = [
-            jnp.where(along_y == at_y + (dy - 1.0), 1.0, 0.0).astype(BF16) for dy in range(3)
-        ]
-        along_z = lax.broadcasted_iota(jnp.int32, (size_z, many), 0).astype(F32)
         for dz in range(3):
-            across[:, dz * many : dz * many + many] = jnp.where(
-                along_z == at_z + (dz - 1.0), 1.0, 0.0
-            ).astype(BF16)
             for s in range(1 if twice else 2):
-                for c in range(4):
-                    for x in range(size_x):
+                for number, x in enumerate(xs):
+                    for c in range(4):
                         total = None
                         for dy in range(3):
                             line = values[s, c, x, 3 * dy + dz : 3 * dy + dz + 1, 0:many]
                             line = jnp.broadcast_to(line, (size_y, many)).astype(BF16)
                             term = ones_y[dy] * line
                             total = term if total is None else total + term
-                        base = ((s * 4 + c) * size_x + x) * size_y
+                        base = s * half + number * block + c * size_y
                         spread[base : base + size_y, dz * many : dz * many + many] = total
-        half = 4 * size_x * size_y
         both = lax.dot_general(
             spread[0 : half if twice else 2 * half, 0 : 3 * many],
             across[:, 0 : 3 * many],
@@ -442,11 +453,11 @@
     solids[...] = deposit(
         table,
         payload[3:4, :],
-        payload[4:5, :],
-        payload[5:6, :],
+        prepare(table, payload[4:5, :], payload[5:6, :]),
         [payload[axis : axis + 1, :] for axis in range(3)],
         planes,
         False,
+        ENDMOST + MIDDLE,
     )
 
     load.wait()
@@ -470,18 +481,22 @@
         when_there(back, lambda number=number: mail(number).wait_recv())
     letters = inbox[...].reshape(64, 128)
     came = jnp.concatenate([letters, letters], axis=0).T
-    solids[...] += deposit(
-        128,
-        came[3:4, :],
-        came[4:5, :],
-        came[5:6, :],
-        [came[axis : axis + 1, :] for axis in range(3)],
-        [came[8 + 16 * plane : 17 + 16 * plane, :] for plane in range(3)],
-        True,
-    )
-
+    came_y = prepare(128, came[4:5, :], came[5:6, :])
+
+    def deposit_came(xs):
+        rows = slice(turned[xs[0]] * block, (turned[xs[-1]] + 1) * block)
+        solids[rows, :] += deposit(
+            128,
+            came[3:4, :],
+            came_y,
+            [came[axis : axis + 1, :] for axis in range(3)],
+            [came[8 + 16 * plane : 17 + 16 * plane, :] for plane in range(3)],
+            True,
+            xs,
+        )
+
+    deposit_came(ENDMOST)
     lane = lax.broadcasted_iota(jnp.int32, (8, 128), 1)
-    plane_rows = size_x * size_y
 
     def rolled(halves, shift):
         turned = [pltpu.roll(half, shift % 128, 1) for half in halves]
@@ -492,10 +507,7 @@
         posts = []
         for h in range(2):
             lanes = slice(128 * h, 128 * h + 128)
-            whole_rows = [
-                pl.ds(pl.multiple_of(c * plane_rows + x * size_y + tile * 8, 8), 8)
-                for c in range(4)
-            ]
+            whole_rows = [rows_of(x, c, tile) for c in range(4)]
             fields = [solids[whole_rows[c], lanes] for c in range(4)]
             if step == 0:
                 own = pl.ds(pl.multiple_of(tile * 8, 8), 8)
@@ -678,18 +690,15 @@
                     :,
                 ]
 
-    def finish(early):
+    def finish(part):
         for number in range(19):
             for x in range(size_x):
-                from_x = 0 <= x - VEL[number][0] < size_x
-                ready = [
-                    tile
-                    for tile in range(tiles)
-                    if from_x
-                    and not (VEL[number][1] == 1 and tile == 0)
-                    and not (VEL[number][1] == -1 and tile == tiles - 1)
-                ]
-                final(number, x, ready if early else [t for t in range(tiles) if t not in ready])
+                inside_x = 0 <= x - VEL[number][0] < size_x
+                needs_row = {1: 0, -1: tiles - 1}.get(VEL[number][1])
+                if part == "faces":
+                    final(number, x, () if inside_x else range(tiles))
+                elif inside_x:
+                    final(number, x, [t for t in range(tiles) if (t == needs_row) == (part == "rows")])
 
     def edges(step, tile, halos=()):
         chunk(step, size_x - 1, tile)
@@ -700,19 +709,20 @@
 
     edges(0, 0, ENDS_DOWN)
     edges(0, tiles - 1, ENDS_UP)
+    deposit_came(MIDDLE)
+
+    lax.fori_loop(0, 4, sweep(0, rims), 0)
+    stage_rows(0)
+    begin(0, ROWS)
 
     @pl.loop(1, tiles - 1)
     def _(turn):
         edges(0, turn)
 
-    lax.fori_loop(0, 4, sweep(0, rims), 0)
-    stage_rows(0)
-    begin(0, ROWS)
     lax.fori_loop(0, 2 * (tiles - 2), sweep(0, inner), 0)
     lax.fori_loop(0, 2 * (tiles - 2), sweep(1, inner), 0)
     arrive(0, ROWS)
     fill_rows(0)
-    lax.fori_loop(0, 4, sweep(1, rims), 0)
     arrive(0, ENDS)
     fill_ends(0)
     face_arrive(0, 0)
@@ -721,6 +731,7 @@
     for piece in range(2, tiles):
         face_arrive(0, piece)
     edges(1, tiles - 1, ENDS_UP)
+    lax.fori_loop(0, 4, sweep(1, rims), 0)
     stage_rows(1)
     begin(1, ROWS)
 
@@ -728,14 +739,15 @@
     def _(turn):
         edges(1, turn)
 
-    finish(True)
+    finish("own")
     arrive(1, ROWS)
     fill_rows(1)
+    finish("rows")
     for piece in range(tiles):
         face_arrive(1, piece)
     arrive(1, ENDS)
     fill_ends(1)
-    finish(False)
+    finish("faces")
     for number, side in enumerate(SIDES):
         when_there(side, lambda number=number: mail(number).wait_send())
     for step in range(2):

time: 25 us -> 24.7 us (0.988)
  Pallas kernels: 23.5 us -> 23.2 us
    pallas_call x1, Pallas kernels: 23.5 us -> 23.2 us  [local(): pl.pallas_call(functools.partial(main_kernel, (size_x, size_y, size_z, ta...]
where the time goes in v4:
time: 24.7 us; the launch traced here: 24.6 us
  Pallas kernels  23.2 us (94%)
  local copies, waits for them, and re-layouts  1.45 us (6%)
    pallas_call x1, Pallas kernels, local(): pl.pallas_call(functools.partial(main_kernel, (size_x, size_y, size_z, ta...  23.2 us
    unnamed x1, local copies, waits for them, and re-layouts  1.45 us

profile of v4, /device:TPU:0, one launch (start us, length us, event | category | flops | bytes accessed | tf_op | source)
XLA Modules:
  0.0 24.6 jit_solution(14022271693726152257)
XLA Ops:
  0.0 23.2 %shard_map.73 = f32[19,4,32,256]{3,2,1,0:T(8,128)S(1)} custom-call(f32[19]{0:T(128)} %rates_hbm.1, f32[3,512]{1,0:T(4,128)} %velocity_hbm.1, f32[3,512]{1,0:T(4,128)} %change_hbm.1, f32[27,512]{1,0:T(8,128)} %fractions_hbm.1, s32[1,512]{1,0:T(1,128)} %bitcast.2, s32[1,512]{1,0:T(1,128)} %bitcast.3, f32[19,4,32,256]{3,2,1,0:T(8,128)} %populations.1), custom_call_target="tpu_custom_call" | custom-call | tf_op jit(solution)/shard_map/pallas_call | solution.py:771
  23.2 1.5 %copy.9 = f32[19,4,32,256]{3,2,1,0:T(8,128)} copy(f32[19,4,32,256]{3,2,1,0:T(8,128)S(1)} %shard_map.73) | data formatting | bytes 4980736

commit v5 on v4

--- a/solution.py
+++ b/solution.py
@@ -504,7 +504,8 @@
         return [jnp.where(edge, turned[1 - h], turned[h]) for h in range(2)]
 
     def chunk(step, x, tile):
-        posts = []
+        out = sent1 if step == 0 else sent2
+        rows = pl.ds(pl.multiple_of(tile * 8 + PAD, 8), 8)
         for h in range(2):
             lanes = slice(128 * h, 128 * h + 128)
             whole_rows = [rows_of(x, c, tile) for c in range(4)]
@@ -532,15 +533,20 @@
                 ]
                 solid, triple = fields[0], fields[1:]
                 density, kept, off = fluid_part(value, lambda number: coef[number])
-            posts.append(solid_part(density, kept, off, solid, triple))
-        out = sent1 if step == 0 else sent2
-        rows = pl.ds(pl.multiple_of(tile * 8 + PAD, 8), 8)
-        for number in range(19):
-            halves = [posts[0][number], posts[1][number]]
-            if VEL[number][2]:
-                halves = rolled(halves, VEL[number][2])
-            for h in range(2):
-                out[SLOT[number], x + 1, h, rows, :] = halves[h]
+            post = solid_part(density, kept, off, solid, triple)
+            for number in range(19):
+                shift = VEL[number][2]
+                if shift:
+                    turned_post = pltpu.roll(post[number], shift % 128, 1)
+                    edge = lane == (0 if shift == 1 else 127)
+                    pltpu.store(
+                        out.at[SLOT[number], x + 1, h, rows, :], turned_post, mask=jnp.logical_not(edge)
+                    )
+                    pltpu.store(
+                        out.at[SLOT[number], x + 1, 1 - h, rows, :], turned_post, mask=edge
+                    )
+                else:
+                    out[SLOT[number], x + 1, h, rows, :] = post[number]
 
     def sweep(step, places):
         def body(turn, carry):

time: 24.7 us -> 24.7 us (level)
  no operation moved by 1% of the time
where the time goes in v5:
time: 24.7 us; the launch traced here: 24.6 us
  Pallas kernels  23.1 us (94%)
  local copies, waits for them, and re-layouts  1.45 us (6%)
    pallas_call x1, Pallas kernels, local(): pl.pallas_call(functools.partial(main_kernel, (size_x, size_y, size_z, ta...  23.1 us
    unnamed x1, local copies, waits for them, and re-layouts  1.45 us

profile of v5, /device:TPU:0, one launch (start us, length us, event | category | flops | bytes accessed | tf_op | source)
XLA Modules:
  0.0 24.6 jit_solution(18395774293457657513)
XLA Ops:
  0.0 23.1 %shard_map.73 = f32[19,4,32,256]{3,2,1,0:T(8,128)S(1)} custom-call(f32[19]{0:T(128)} %rates_hbm.1, f32[3,512]{1,0:T(4,128)} %velocity_hbm.1, f32[3,512]{1,0:T(4,128)} %change_hbm.1, f32[27,512]{1,0:T(8,128)} %fractions_hbm.1, s32[1,512]{1,0:T(1,128)} %bitcast.2, s32[1,512]{1,0:T(1,128)} %bitcast.3, f32[19,4,32,256]{3,2,1,0:T(8,128)} %populations.1), custom_call_target="tpu_custom_call" | custom-call | tf_op jit(solution)/shard_map/pallas_call | solution.py:777
  23.1 1.5 %copy.9 = f32[19,4,32,256]{3,2,1,0:T(8,128)} copy(f32[19,4,32,256]{3,2,1,0:T(8,128)S(1)} %shard_map.73) | data formatting | bytes 4980736

commit v6 on v5

--- a/solution.py
+++ b/solution.py
@@ -607,10 +607,6 @@
                 lambda kind=kind, number=number: halo(step, kind, number).wait_recv(),
             )
 
-    def face_begin(step, piece):
-        for number in range(2):
-            halo(step, "x", number, piece).start()
-
     def face_arrive(step, piece):
         for number in range(2):
             halo(step, "x", number, piece).wait_recv()
@@ -708,10 +704,11 @@
 
     def edges(step, tile, halos=()):
         chunk(step, size_x - 1, tile)
+        halo(step, "x", 0, tile).start()
         chunk(step, 0, tile)
         stage_ends(step, halos)
         begin(step, halos)
-        face_begin(step, tile)
+        halo(step, "x", 1, tile).start()
 
     edges(0, 0, ENDS_DOWN)
     edges(0, tiles - 1, ENDS_UP)

time: 24.7 us -> 24.9 us (level)
  no operation moved by 1% of the time
where the time goes in v6:
time: 24.9 us; the launch traced here: 24.8 us
  Pallas kernels  23.3 us (94%)
  local copies, waits for them, and re-layouts  1.45 us (6%)
    pallas_call x1, Pallas kernels, local(): pl.pallas_call(functools.partial(main_kernel, (size_x, size_y, size_z, ta...  23.3 us
    unnamed x1, local copies, waits for them, and re-layouts  1.45 us

profile of v6, /device:TPU:0, one launch (start us, length us, event | category | flops | bytes accessed | tf_op | source)
XLA Modules:
  0.0 24.8 jit_solution(265108577524797821)
XLA Ops:
  0.0 23.3 %shard_map.73 = f32[19,4,32,256]{3,2,1,0:T(8,128)S(1)} custom-call(f32[19]{0:T(128)} %rates_hbm.1, f32[3,512]{1,0:T(4,128)} %velocity_hbm.1, f32[3,512]{1,0:T(4,128)} %change_hbm.1, f32[27,512]{1,0:T(8,128)} %fractions_hbm.1, s32[1,512]{1,0:T(1,128)} %bitcast.2, s32[1,512]{1,0:T(1,128)} %bitcast.3, f32[19,4,32,256]{3,2,1,0:T(8,128)} %populations.1), custom_call_target="tpu_custom_call" | custom-call | tf_op jit(solution)/shard_map/pallas_call | solution.py:774
  23.3 1.5 %copy.9 = f32[19,4,32,256]{3,2,1,0:T(8,128)} copy(f32[19,4,32,256]{3,2,1,0:T(8,128)S(1)} %shard_map.73) | data formatting | bytes 4980736

commit v7 on v5

--- a/solution.py
+++ b/solution.py
@@ -321,13 +321,13 @@
     ]
     for fetch in fetches:
         fetch.start()
-    load = pltpu.make_async_copy(populations, start, load_sem)
-    load.start()
 
     payload[...] = jnp.zeros_like(payload)
     outbox[...] = jnp.zeros_like(outbox)
     for fetch in fetches:
         fetch.wait()
+    load = pltpu.make_async_copy(populations, start, load_sem)
+    load.start()
     place = anchor[...]
     place_x = lax.shift_right_logical(place, 13)
     place_y = lax.bitwise_and(lax.shift_right_logical(place, 8), 31)

time: 24.7 us -> 24.7 us (level)
  no operation moved by 1% of the time
where the time goes in v7:
time: 24.7 us; the launch traced here: 24.6 us
  Pallas kernels  23.1 us (94%)
  local copies, waits for them, and re-layouts  1.45 us (6%)
    pallas_call x1, Pallas kernels, local(): pl.pallas_call(functools.partial(main_kernel, (size_x, size_y, size_z, ta...  23.1 us
    unnamed x1, local copies, waits for them, and re-layouts  1.45 us

profile of v7, /device:TPU:0, one launch (start us, length us, event | category | flops | bytes accessed | tf_op | source)
XLA Modules:
  0.0 24.6 jit_solution(9250426532604665527)
XLA Ops:
  0.0 23.1 %shard_map.73 = f32[19,4,32,256]{3,2,1,0:T(8,128)S(1)} custom-call(f32[19]{0:T(128)} %rates_hbm.1, f32[3,512]{1,0:T(4,128)} %velocity_hbm.1, f32[3,512]{1,0:T(4,128)} %change_hbm.1, f32[27,512]{1,0:T(8,128)} %fractions_hbm.1, s32[1,512]{1,0:T(1,128)} %bitcast.2, s32[1,512]{1,0:T(1,128)} %bitcast.3, f32[19,4,32,256]{3,2,1,0:T(8,128)} %populations.1), custom_call_target="tpu_custom_call" | custom-call | tf_op jit(solution)/shard_map/pallas_call | solution.py:777
  23.1 1.5 %copy.9 = f32[19,4,32,256]{3,2,1,0:T(8,128)} copy(f32[19,4,32,256]{3,2,1,0:T(8,128)S(1)} %shard_map.73) | data formatting | bytes 4980736
